TPU v7x, 256 devices: a whole 4x4x8 slice. The times are simulated.
256 devices in a mesh: img: 64 (over x, z, core), tpa: 2 (over y_lo), tpb: 2 (over y_hi).
Axes of the slice: x: 4, y: 4 (y_hi: 2, y_lo: 2; y = y_hi * 2 + y_lo), z: 8, core: 2. Of those that a mesh axis runs over, the one named last changes fastest.
Arguments:
- images: bfloat16 [8192, 512], P('img'), may hold values from -80 to 80
- templates: bfloat16 [16384, 512], P(('tpa', 'tpb')), may hold values from -8 to 8
- rotation_index: int32 [16384], P(('tpa', 'tpb')), may hold values from 0 to 31
- tilt_index: int32 [16384], P(('tpa', 'tpb')), may hold values from 0 to 63
- inplane_index: int32 [16384], P(('tpa', 'tpb')), may hold values from 0 to 31
- image_group: int32 [8192], P('img'), may hold values from 0 to 15
- group_precision: float32 [16], replicated, may hold values from 0.5 to 2
- radius_bin: int32 [8], replicated, may hold values from 0 to 3
Outputs:
- shell_coeffs: float32 [32, 4, 2, 49], replicated
- image_loglik: float32 [8192], P('img')
All inputs are finite; a program needn't handle non-finite values.
Results may differ from a plain program's by a relative error of at most 0.0024.
Values sent between devices are 32-bit elements; how exact they have to be, the bound alone decides.
A program may use at most 64 MiB of HBM per device.

v0:
```python
import math

import jax
import jax.numpy as jnp
from jax import lax
from jax.sharding import PartitionSpec as P

TEMPLATES = 16384
ORDERS = 32
RADII = 8
LDEG = 48
SHELLS = 4
NTILT = 64
NROT = 32
NPSI = 32
NGROUP = 16


RIDGE = 0.05


def legendre_table():
    angles = jnp.pi * (jnp.arange(NTILT, dtype=jnp.float32) + 0.5) / NTILT
    cosine = jnp.cos(angles)[:, None]
    sine_vals = jnp.sin(angles)
    orders_f = jnp.arange(ORDERS, dtype=jnp.float32)[None, :]
    diagonal = [jnp.full((NTILT,), (4.0 * math.pi) ** (-0.5), jnp.float32)]
    for step_m in range(1, ORDERS):
        diagonal.append(-math.sqrt((2 * step_m + 1) / (2.0 * step_m)) * sine_vals * diagonal[-1])
    corner = jnp.stack(diagonal, axis=1)
    before = jnp.zeros((NTILT, ORDERS), jnp.float32)
    latest = jnp.zeros((NTILT, ORDERS), jnp.float32)
    columns = []
    for degree in range(LDEG + 1):
        degree_f = float(degree)
        lower_f = float(degree - 1)
        factor = jnp.sqrt(
            max(4.0 * degree_f * degree_f - 1.0, 1.0)
            / jnp.maximum(degree_f * degree_f - orders_f * orders_f, 1.0)
        )
        factor_prev = jnp.sqrt(
            max(4.0 * lower_f * lower_f - 1.0, 1.0)
            / jnp.maximum(lower_f * lower_f - orders_f * orders_f, 1.0)
        )
        recurred = factor * (cosine * latest - before / factor_prev)
        current = jnp.where(
            orders_f == degree_f, corner, jnp.where(orders_f < degree_f, recurred, 0.0)
        )
        columns.append(current)
        before, latest = (latest, current)
    return jnp.stack(columns, axis=2)


def back_project(columns, col_start, angles, tilt_hot, radius_bin, shell_table):
    pair_count = columns.shape[0] // 2
    paired = columns.reshape(pair_count, 2, columns.shape[1])
    pair_ids = col_start // 2 + jnp.arange(pair_count, dtype=jnp.int32)
    order_ids = pair_ids // RADII
    radial = pair_ids % RADII
    phases = order_ids.astype(jnp.float32)[:, None] * angles[None, :]
    cosine = jnp.cos(phases)
    sine_vals = jnp.sin(phases)
    real_y = paired[:, 0] * cosine + paired[:, 1] * sine_vals
    imag_y = paired[:, 1] * cosine - paired[:, 0] * sine_vals
    binned = jnp.dot(
        jnp.concatenate([real_y, imag_y], axis=0), tilt_hot, precision=lax.Precision.HIGHEST
    )
    order_hot = (order_ids[:, None] == jnp.arange(ORDERS, dtype=jnp.int32)[None, :]).astype(
        jnp.float32
    )
    picked = jnp.einsum("po,kol->pkl", order_hot, shell_table, precision=lax.Precision.HIGHEST)
    real_q = jnp.einsum("pk,pkl->pl", binned[:pair_count], picked, precision=lax.Precision.HIGHEST)
    imag_q = jnp.einsum("pk,pkl->pl", binned[pair_count:], picked, precision=lax.Precision.HIGHEST)
    radial_hot = radial[:, None] == jnp.arange(RADII, dtype=jnp.int32)[None, :]
    shells = jnp.sum(jnp.where(radial_hot, radius_bin[None, :], 0), axis=1)
    target = order_ids * SHELLS + shells
    target_hot = (target[:, None] == jnp.arange(ORDERS * SHELLS, dtype=jnp.int32)[None, :]).astype(
        jnp.float32
    )
    real_b = jnp.einsum("pg,pl->gl", target_hot, real_q, precision=lax.Precision.HIGHEST)
    imag_b = jnp.einsum("pg,pl->gl", target_hot, imag_q, precision=lax.Precision.HIGHEST)
    return jnp.stack([real_b, imag_b], axis=1).reshape(ORDERS, SHELLS, 2, LDEG + 1)


def solve_shells(right_side, bin_mass, radius_bin, shell_table):
    shell_hot = (radius_bin[:, None] == jnp.arange(SHELLS, dtype=jnp.int32)[None, :]).astype(
        jnp.float32
    )
    counts = jnp.sum(shell_hot, axis=0)
    massed = bin_mass[:, None, None] * shell_table
    normal_m = jnp.einsum("kol,koj->olj", massed, shell_table, precision=lax.Precision.HIGHEST)
    ridge_term = RIDGE * jnp.mean(bin_mass)
    identity = jnp.eye(LDEG + 1, dtype=jnp.float32)
    gram = (
        counts[None, :, None, None] * normal_m[:, None]
        + (ridge_term * (counts + 1.0))[None, :, None, None] * identity
    )
    factor = jnp.linalg.cholesky(gram)
    solver = jax.vmap(
        jax.vmap(
            lambda factor_one, right_one: jax.scipy.linalg.cho_solve((factor_one, True), right_one)
        )
    )
    solved = solver(factor, jnp.swapaxes(right_side, 2, 3))
    return jnp.swapaxes(solved, 2, 3) * math.sqrt(TEMPLATES)


def body(
    images,
    templates,
    rotation_index,
    tilt_index,
    inplane_index,
    image_group,
    group_precision,
    radius_bin,
):
    coef_count = images.shape[1]
    tpl_f = templates.astype(jnp.float32)
    half_norm = 0.5 * jnp.sum(tpl_f * tpl_f, axis=1)
    group_hot = image_group[:, None] == jnp.arange(NGROUP, dtype=jnp.int32)[None, :]
    weights_img = jnp.sum(
        jnp.where(group_hot, group_precision[None, :], 0.0), axis=1
    ) * coef_count ** (-0.5)
    raw_dot = lax.dot_general(
        images, templates, (((1,), (1,)), ((), ())), preferred_element_type=jnp.float32
    )
    scores = (raw_dot - half_norm[None, :]) * weights_img[:, None]
    local_top = jnp.max(scores, axis=1)
    top_score = lax.pmax(local_top, ("tpa", "tpb"))
    exp_total = lax.psum(jnp.sum(jnp.exp(scores - top_score[:, None]), axis=1), ("tpa", "tpb"))
    log_total = top_score + jnp.log(exp_total)
    post_full = jnp.exp(scores - log_total[:, None])
    posterior = post_full.astype(jnp.bfloat16)
    tilt_hot = (tilt_index[:, None] == jnp.arange(NTILT, dtype=jnp.int32)[None, :]).astype(
        jnp.float32
    )
    bin_mass = jnp.dot(jnp.sum(post_full, axis=0), tilt_hot, precision=lax.Precision.HIGHEST)
    angles = (
        2.0
        * jnp.pi
        * (rotation_index.astype(jnp.float32) / NROT + inplane_index.astype(jnp.float32) / NPSI)
    )
    shell_table = legendre_table()
    col_count = coef_count // lax.axis_size("img")
    summed = lax.psum_scatter(
        lax.dot_general(
            images, posterior, (((0,), (0,)), ((), ())), preferred_element_type=jnp.float32
        ),
        "img",
        scatter_dimension=0,
        tiled=True,
    )
    right_side = back_project(
        summed, lax.axis_index("img") * col_count, angles, tilt_hot, radius_bin, shell_table
    )
    right_all, mass_all = lax.psum((right_side, bin_mass), ("img", "tpa", "tpb"))
    return (solve_shells(right_all, mass_all, radius_bin, shell_table), log_total)


def solution(mesh):
    in_specs = (
        P("img", None),
        P(("tpa", "tpb"), None),
        P(("tpa", "tpb")),
        P(("tpa", "tpb")),
        P(("tpa", "tpb")),
        P("img"),
        P(),
        P(),
    )
    out_specs = (P(), P("img"))
    return jax.shard_map(body, mesh=mesh, in_specs=in_specs, out_specs=out_specs, check_vma=False)
```

profile of v0, /device:TPU:1, one launch (start us, length us, event | category | flops | bytes accessed | tf_op | source)
XLA Modules:
  0.0 1050.0 jit_solution(14513425907578487953)
XLA Ops:
  7.2 0.9 select_reduce_fusion.1
  8.2 3.3 multiply_reduce_fusion
  11.5 1.6 fusion.44
  13.0 9.8 pmax.7
  23.3 7.2 psum.21
  31.1 4.7 convolution_bitcast_fusion
  35.8 9.0 copy.141
  49.6 1.5 select_select_fusion
  51.1 4.4 broadcast_select_fusion
  55.6 3.7 stack.261
  59.3 0.8 convert_reduce_fusion
  60.1 0.8 select_reduce_fusion.2
  61.0 1.0 fusion.4
  62.0 1.7 fusion.7
  63.7 0.7 add_multiply_fusion.1
  64.9 133.4 %reduce-scatter.4.cloned.1.call-done = f32[8,4096]{1,0:T(8,128)} async-done(((f32[512,4096]{1,0:T(8,128)}), f32[8,4096]{1,0:T(8,128)}) %reduce-scatter.4.cloned.1.call-update) | async-done | bytes 131088 | tf_op jit(solution)/shard_map/reduce_scatter | solution.py:146
  198.3 1.0 reshape.71240
  199.4 0.6 fusion.26
  200.0 1.0 fusion.1
  202.4 80.3 %all-reduce = (f32[64]{0:T(128)S(1)}, f32[32,4,2,49]{3,2,1,0:T(2,128)S(1)}) all-reduce(f32[64]{0:T(128)S(1)} %fusion.7, f32[32,4,2,49]{3,2,1,0:T(2,128)S(1)} %pad_maximum_fusion), channel_id=1, replica_groups=mesh['img'=64,'tpa'=2,'tpb'=2] {'img','tpa','tpb'}, use_global_device_ids=true, to_apply=%region_8.9 | all-reduce | flops 12608 | bytes 100864 | tf_op jit(solution)/shard_map/psum | solution.py:157
  282.7 1.6 fusion.5
  284.3 0.6 reduce_sum.68
  286.1 2.6 add_multiply_fusion
  288.7 577.0 %custom-call.11 = f32[32,4,49,49]{3,2,1,0:T(8,128)} custom-call(f32[32,4,49,49]{3,2,1,0:T(8,128)} %add_multiply_fusion), custom_call_target="Cholesky" | custom-call | tf_op jit(solution)/shard_map/jit(cholesky)/cholesky | solution.py:98
  865.7 5.9 copy.124
  871.6 3.2 select_reduce_fusion
  874.9 1.0 copy-done.1
  875.9 2.9 select_bitcast_fusion
  878.7 147.0 %custom-call.12 = f32[32,4,1,49,49]{0,3,4,2,1:T(8,128)} custom-call(f32[32,4,1,49,49]{0,4,3,2,1:T(8,128)} %select_bitcast_fusion), custom_call_target="InvertDiagBlocksLowerTriangular" | custom-call | tf_op jit(solution)/shard_map/vmap(vmap(jit(_cho_solve)))/triangular_solve | solution.py:101
  1025.7 5.9 copy.132
  1031.6 7.6 fusion.45
  1039.2 4.0 convolution_multiply_fusion
  (160 shorter events, 8.0 us)
Async XLA Ops:
  7.2 4.3 copy-start
  7.2 191.1 %reduce-scatter.4.cloned.1.call-start = ((), (), s32[]{:S(2)}) async-start(), calls=%async_computation.1 | async-start | bytes 8519680 | tf_op jit(solution)/shard_map/reduce_scatter | solution.py:146
  7.2 4.3 copy-start.3
  30.6 0.5 copy-start.4
  59.3 140.7 %copy-start.5 = (s32[4096]{0:T(1024)S(1)}, s32[4096]{0:T(1024)}, u32[]{:S(2)}) copy-start(s32[4096]{0:T(1024)} %param.11) | copy-start | bytes 49156
  871.6 4.3 copy-start.1
  1031.6 7.6 copy-start.2
Sparse Core Ops, SparseCore 0:
  44.9 153.2 reduce-scatter.3
where the time goes:
time: 1050 us
  other arithmetic  752 us (72%)
  waiting for transfers between devices  133 us (13%)
  blocking collectives  97.4 us (9%)
  local copies, waits for them, and re-layouts  27.7 us (3%)
  matrix products  23.8 us (2%)
  between operations  15.3 us (1%)
    another operation x4, other arithmetic, solve_shells(): factor = jnp.linalg.cholesky(gram)  580 us
    another operation x3, other arithmetic, solve_shells(): jax.scipy.linalg.cho_solve((factor_one, True), right_one)  150 us
    reduce_scatter x1, waiting for transfers between devices, body(): lax.psum_scatter(lax.dot_general(images, posterior, (((0,), (0,)), ((), (...  133 us
    psum x1, blocking collectives, body(): lax.psum((right_side, bin_mass), ('img', 'tpa', 'tpb'))  80.3 us
  transfers between devices with their start and end apart: 1, of which 1 were waited for; matrix products, arithmetic and copies ran while one was open for 2% of the time, Pallas kernels for 0%

commit v1 on v0

v1 whole, which is shorter than its diff:
```python
import functools
import math

import jax
import jax.numpy as jnp
import numpy as np
from jax import lax
from jax.experimental import pallas as pl
from jax.experimental.pallas import tpu as pltpu
from jax.sharding import PartitionSpec as P

TEMPLATES = 16384
ORDERS = 32
RADII = 8
COEFS = 512
LDEG = 48
SHELLS = 4
NTILT = 64
NROT = 32
NGROUP = 16
RIDGE = 0.05

NX, NZ, NCORE, NY = 4, 8, 2, 4
NYC = NY * NCORE
LANES = 128
LB = 7
LPAD = 8 * LB
LROWS = LDEG + 1
CHUNK = 256
F32, BF16, I32 = jnp.float32, jnp.bfloat16, jnp.int32
MESH = pl.DeviceIdType.MESH


def legendre_table():
    theta = np.pi * (np.arange(NTILT) + 0.5) / NTILT
    cosine, sine = np.cos(theta)[:, None], np.sin(theta)
    orders = np.arange(ORDERS, dtype=np.float64)[None, :]
    diagonal = [np.full((NTILT,), (4.0 * np.pi) ** -0.5)]
    for m in range(1, ORDERS):
        diagonal.append(-np.sqrt((2 * m + 1) / (2.0 * m)) * sine * diagonal[-1])
    corner = np.stack(diagonal, axis=1)
    before = np.zeros((NTILT, ORDERS))
    latest = np.zeros((NTILT, ORDERS))
    columns = []
    for degree in range(LDEG + 1):
        low = float(degree - 1)
        factor = np.sqrt(
            max(4.0 * degree * degree - 1.0, 1.0)
            / np.maximum(degree * degree - orders * orders, 1.0)
        )
        factor_prev = np.sqrt(
            max(4.0 * low * low - 1.0, 1.0) / np.maximum(low * low - orders * orders, 1.0)
        )
        recurred = factor * (cosine * latest - before / factor_prev)
        current = np.where(orders == degree, corner, np.where(orders < degree, recurred, 0.0))
        columns.append(current)
        before, latest = latest, current
    return np.stack(columns, axis=2)


def constant_tables():
    legendre = legendre_table().transpose(0, 2, 1)
    padded = np.zeros((NTILT, LPAD, ORDERS))
    padded[:, :LROWS] = legendre
    spread = np.tile(padded, (1, 1, SHELLS)).astype(np.float32)
    quarter = NTILT // 4
    packed = np.concatenate([padded[q * quarter : (q + 1) * quarter] for q in range(4)], axis=2)
    packed = packed.astype(np.float32)
    step = np.arange(NROT)[:, None] * np.arange(ORDERS)[None, :] % NROT
    turn = 2.0 * np.pi * step / NROT
    both = np.concatenate([np.tile(np.cos(turn), (1, 4)), np.tile(np.sin(turn), (1, 4))], axis=1)
    rest, terms = both, []
    for _ in range(3):
        term = rest.astype(np.float32).astype(jnp.bfloat16)
        terms.append(term)
        rest = rest - term.astype(np.float64)
    terms.append(np.zeros_like(terms[0]))
    phases = np.concatenate(terms, axis=0)
    return spread, packed, phases


def split2(value):
    high = value.astype(BF16)
    return high, (value - high.astype(F32)).astype(BF16)


def dot(a, b):
    return lax.dot_general(a, b, (((1,), (0,)), ((), ())), preferred_element_type=F32)


def dot_t(a, b):
    return lax.dot_general(a, b, (((1,), (1,)), ((), ())), preferred_element_type=F32)


def kernel(
    tilt_ref,
    rot_ref,
    inp_ref,
    group_ref,
    prec_ref,
    bin_ref,
    phase_ref,
    images_ref,
    lt_hbm,
    lq_hbm,
    templates_hbm,
    out_ref,
    loglik_ref,
    tpl,
    lt,
    lq,
    mlq,
    e_ref,
    ph_ref,
    emass,
    angle_t,
    cmax,
    a_ref,
    w_ref,
    pf_ref,
    dinv,
    bins_ref,
    rhs_ref,
    st_buf,
    m_yc,
    m_x,
    m_z,
    r_yc,
    r_x,
    r_z,
    r_ag,
    tpl_sem,
    tab_sem,
    st_send,
    st_recv,
    myc_send,
    myc_recv,
    mx_send,
    mx_recv,
    mz_send,
    mz_recv,
    ryc_send,
    ryc_recv,
    rx_send,
    rx_recv,
    rz_send,
    rz_recv,
    rag_send,
    rag_recv,
):
    t_count = templates_hbm.shape[0]
    chunks = t_count // CHUNK
    img = lax.axis_index("img")
    tpa = lax.axis_index("tpa")
    tpb = lax.axis_index("tpb")
    core = lax.rem(img, NCORE)
    zpos = lax.rem(lax.div(img, NCORE), NZ)
    xpos = lax.div(img, NCORE * NZ)
    ypos = tpa * 2 + tpb
    ycpos = ypos * NCORE + core

    def at_y(p):
        return {"img": img, "tpa": lax.div(p, 2), "tpb": lax.rem(p, 2)}

    def at_yc(p):
        y = lax.div(p, NCORE)
        return {
            "img": lax.div(img, NCORE) * NCORE + lax.rem(p, NCORE),
            "tpa": lax.div(y, 2),
            "tpb": lax.rem(y, 2),
        }

    def at_x(p):
        return {"img": p * (NZ * NCORE) + lax.rem(img, NZ * NCORE), "tpa": tpa, "tpb": tpb}

    def at_z(p):
        return {
            "img": lax.div(img, NZ * NCORE) * (NZ * NCORE) + p * NCORE + core,
            "tpa": tpa,
            "tpb": tpb,
        }

    def peers(n, me):
        return [lax.rem(me + d, n) for d in range(1, n)]

    def remote(src, dst, send, recv, device):
        return pltpu.make_async_remote_copy(
            src_ref=src,
            dst_ref=dst,
            send_sem=send,
            recv_sem=recv,
            device_id=device,
            device_id_type=MESH,
        )

    def share(buf, send, recv, n, me, at):
        for d, p in enumerate(peers(n, me)):
            remote(buf.at[me], buf.at[me], send.at[d], recv.at[me], at(p)).start()

    def shared(buf, send, recv, n, me, at):
        for d, p in enumerate(peers(n, me)):
            remote(buf.at[p], buf.at[p], send.at[d], recv.at[p], at(p)).wait_recv()

    def sent(buf, send, recv, n, me, at):
        for d, p in enumerate(peers(n, me)):
            remote(buf.at[me], buf.at[me], send.at[d], recv.at[me], at(p)).wait_send()

    barrier = pltpu.get_barrier_semaphore()
    for n, me, at in ((NYC, ycpos, at_yc), (NX, xpos, at_x), (NZ, zpos, at_z)):
        for p in peers(n, me):
            pl.semaphore_signal(barrier, inc=1, device_id=at(p), device_id_type=MESH)

    def tpl_copy(b):
        rows = pl.ds(pl.multiple_of(b * CHUNK, CHUNK), CHUNK)
        return pltpu.make_async_copy(templates_hbm.at[rows], tpl.at[rows], tpl_sem.at[b])

    for b in range(chunks):
        tpl_copy(b).start()
    lt_copy = pltpu.make_async_copy(lt_hbm, lt, tab_sem.at[0])
    lq_copy = pltpu.make_async_copy(lq_hbm, lq, tab_sem.at[1])
    lt_copy.start()
    lq_copy.start()

    lane = lax.broadcasted_iota(I32, (1, LANES), 1)

    group = group_ref[...]
    weight = jnp.zeros((1, LANES), F32)
    for g in range(NGROUP):
        weight = jnp.where(group == g, prec_ref[g], weight)
    weight = weight * (COEFS ** -0.5)

    c_id = lax.broadcasted_iota(I32, (COEFS, LANES), 0)
    radial = lax.rem(lax.div(c_id, 2), RADII)
    shell_of = jnp.zeros((COEFS, LANES), I32)
    for p in range(RADII):
        shell_of = jnp.where(radial == p, bin_ref[p], shell_of)
    column = shell_of * ORDERS + lax.div(c_id, 2 * RADII)
    hit = column == lax.broadcasted_iota(I32, (COEFS, LANES), 1)
    part_of = lax.rem(c_id, 2)
    select = jnp.concatenate(
        [
            jnp.where(jnp.logical_and(hit, part_of == 0), 1.0, 0.0),
            jnp.where(jnp.logical_and(hit, part_of == 1), 1.0, 0.0),
        ],
        axis=1,
    ).astype(BF16)
    images = images_ref[...]
    img_high, img_low = split2(dot(images, select))
    shelled = jnp.concatenate([img_high, img_low], axis=0)

    angle = lax.rem(rot_ref[...] + inp_ref[...], NROT).astype(F32)
    rows_t = angle.shape[0]
    angle = jnp.concatenate([angle, jnp.zeros((LANES - rows_t, LANES), F32)], axis=0)
    angle_t[...] = angle.T

    def score_chunk(b, _):
        tpl_copy(b).wait()
        rows = pl.ds(pl.multiple_of(b * CHUNK, CHUNK), CHUNK)
        block = tpl[rows, :]
        raw = dot_t(block, images)
        wide = block.astype(F32)
        half = 0.5 * jnp.sum(wide * wide, axis=1, keepdims=True)
        score = (raw - half) * weight
        top = jnp.max(score, axis=0, keepdims=True)
        e = jnp.exp(score - top)
        e_ref[rows, :] = e
        cmax[pl.ds(b, 1), :] = top
        cmax[pl.ds(chunks + b, 1), :] = jnp.sum(e, axis=0, keepdims=True)
        return 0

    lax.fori_loop(0, chunks, score_chunk, 0)

    tops = cmax[pl.ds(0, chunks), :]
    sums = cmax[pl.ds(chunks, chunks), :]
    top = jnp.max(tops, axis=0, keepdims=True)
    total = jnp.sum(sums * jnp.exp(tops - top), axis=0, keepdims=True)
    row8 = lax.broadcasted_iota(I32, (8, LANES), 0)
    st_buf[ypos] = jnp.where(row8 == 0, top, total)

    pl.semaphore_wait(barrier, (NYC - 1) + (NX - 1) + (NZ - 1))
    share(st_buf, st_send, st_recv, NY, ypos, at_y)

    def tilt_hot(b):
        tilt = jnp.concatenate(
            [tilt_ref[pl.ds(2 * b, 1), :], tilt_ref[pl.ds(2 * b + 1, 1), :]], axis=1
        )
        k_id = lax.broadcasted_iota(I32, (NTILT, CHUNK), 0)
        return jnp.where(k_id == tilt, 1.0, 0.0).astype(BF16)

    lane_sq = lax.broadcasted_iota(I32, (LANES, LANES), 1)

    def prepare_chunk(b, _):
        rows = pl.ds(pl.multiple_of(b * CHUNK, CHUNK), CHUNK)
        hots = []
        for h in range(2):
            picked = jnp.sum(
                jnp.where(lane_sq == 2 * b + h, angle_t[...], 0.0), axis=1, keepdims=True
            )
            hots.append(
                jnp.where(lax.rem(lane_sq, NROT) == picked.astype(I32), 1.0, 0.0).astype(BF16)
            )
        ph_ref[rows, :] = dot(jnp.concatenate(hots, axis=0), phase_ref[...])
        e_high, e_low = split2(e_ref[rows, :])
        both = dot(tilt_hot(b), jnp.concatenate([e_high, e_low], axis=1))
        emass[b] = both[:, :LANES] + both[:, LANES:]
        return 0

    lax.fori_loop(0, chunks, prepare_chunk, 0)

    shared(st_buf, st_send, st_recv, NY, ypos, at_y)
    stats = [st_buf[p] for p in range(NY)]
    all_top = functools.reduce(jnp.maximum, [s[0:1] for s in stats])
    all_sum = functools.reduce(
        jnp.add, [s[1:2] * jnp.exp(s[0:1] - all_top) for s in stats]
    )
    loglik = all_top + jnp.log(all_sum)
    loglik_ref[...] = loglik
    scales = jnp.exp(tops - loglik)
    cmax[pl.ds(0, chunks), :] = scales

    mass = jnp.zeros((NTILT, LANES), F32)
    for b in range(chunks):
        mass = mass + emass[b] * scales[b : b + 1]
    mass = jnp.broadcast_to(jnp.sum(mass, axis=1, keepdims=True), (NTILT, LANES))
    packed = jnp.zeros((8, LANES), F32)
    for a in range(8):
        packed = jnp.where(lax.div(lane, 16) == a, mass[8 * a : 8 * a + 8], packed)
    m_yc[ycpos] = packed
    share(m_yc, myc_send, myc_recv, NYC, ycpos, at_yc)

    bins_ref[...] = jnp.zeros_like(bins_ref)

    def post_chunk(b, _):
        rows = pl.ds(pl.multiple_of(b * CHUNK, CHUNK), CHUNK)
        posterior = (e_ref[rows, :] * cmax[pl.ds(b, 1), :]).astype(BF16)
        weighted = dot(jnp.concatenate([posterior, posterior], axis=1), shelled)
        real, imag = weighted[:, :LANES], weighted[:, LANES:]
        cosine, sine = ph_ref[rows, :LANES], ph_ref[rows, LANES:]
        rotated = jnp.concatenate(
            [real * cosine + imag * sine, imag * cosine - real * sine], axis=1
        )
        high, low = split2(rotated)
        hot = tilt_hot(b)
        both = dot(hot, high) + dot(hot, low)
        bins_ref[0] += both[:, :LANES]
        bins_ref[1] += both[:, LANES:]
        return 0

    half_way = chunks // 2
    lax.fori_loop(0, half_way, post_chunk, 0)

    shared(m_yc, myc_send, myc_recv, NYC, ycpos, at_yc)
    m_x[xpos] = functools.reduce(jnp.add, [m_yc[p] for p in range(NYC)])
    share(m_x, mx_send, mx_recv, NX, xpos, at_x)

    lax.fori_loop(half_way, chunks, post_chunk, 0)

    shared(m_x, mx_send, mx_recv, NX, xpos, at_x)
    m_z[zpos] = functools.reduce(jnp.add, [m_x[p] for p in range(NX)])
    share(m_z, mz_send, mz_recv, NZ, zpos, at_z)

    lt_copy.wait()

    def project(k8, accs):
        accs = list(accs)
        for dk in range(8):
            k = k8 * 8 + dk
            for part in range(2):
                row = bins_ref[part, pl.ds(k, 1), :]
                for jb in range(LB):
                    accs[part * LB + jb] = (
                        accs[part * LB + jb] + lt[k, 8 * jb : 8 * jb + 8, :] * row
                    )
        return tuple(accs)

    zero = jnp.zeros((8, LANES), F32)
    accs = lax.fori_loop(0, NTILT // 8, project, (zero,) * (2 * LB))
    for q in range(2 * NYC):
        rhs_ref[q // 2, (q % 2) * 8 : (q % 2) * 8 + 8, :] = accs[q] if q < 2 * LB else zero

    r_yc[ycpos] = rhs_ref[ycpos]
    for d, p in enumerate(peers(NYC, ycpos)):
        remote(
            rhs_ref.at[p], r_yc.at[ycpos], ryc_send.at[d], ryc_recv.at[ycpos], at_yc(p)
        ).start()

    lq_copy.wait()
    sub8 = lax.broadcasted_iota(I32, (8, LANES), 0)
    for jb in range(LB):
        for ib in range(LB):
            if jb <= ib:
                for r in range(8 if ib < LB - 1 else 1):
                    w_ref[ib * 8 + r, 8 * jb : 8 * jb + 8, :] = (
                        jnp.where(sub8 == r, 1.0, 0.0) if ib == jb else zero
                    )

    shared(r_yc, ryc_send, ryc_recv, NYC, ycpos, at_yc)
    r_x[xpos] = functools.reduce(jnp.add, [r_yc[p] for p in range(NYC)])
    share(r_x, rx_send, rx_recv, NX, xpos, at_x)

    shared(m_z, mz_send, mz_recv, NZ, zpos, at_z)
    pm = functools.reduce(jnp.add, [m_z[p] for p in range(NZ)])
    mean_mass = jnp.sum(jnp.sum(pm, axis=0, keepdims=True), axis=1, keepdims=True) / (
        16.0 * NTILT
    )
    first_half = lax.rem(lane, 32) < 16
    mass_h = (
        jnp.where(first_half, pm, pltpu.roll(pm, 16, 1)),
        jnp.where(first_half, pltpu.roll(pm, LANES - 16, 1), pm),
    )
    shell_lane = lax.div(lane, ORDERS)
    count = jnp.zeros((1, LANES), F32)
    for p in range(RADII):
        count = count + jnp.where(shell_lane == bin_ref[p], 1.0, 0.0)
    ridge = (RIDGE * mean_mass) * (count + 1.0)
    quarter = NTILT // 4
    for k in range(quarter):
        for jb in range(LB):
            mlq[k, 8 * jb : 8 * jb + 8, :] = (
                lq[k, 8 * jb : 8 * jb + 8, :] * mass_h[k // 8][k % 8 : k % 8 + 1]
            )
    for ib in range(LB):

        def gram_row(r, _, ib=ib):
            i = ib * 8 + r
            acc = [zero] * LB
            for k in range(quarter):
                row = mlq[k, pl.ds(i, 1), :]
                for jb in range(ib, LB):
                    acc[jb] = acc[jb] + lq[k, 8 * jb : 8 * jb + 8, :] * row
            for jb in range(ib, LB):
                v = acc[jb]
                v = v + pltpu.roll(v, 32, 1)
                v = v + pltpu.roll(v, 64, 1)
                v = v * count
                if jb == ib:
                    v = v + jnp.where(sub8 == r, ridge, 0.0)
                a_ref[i, 8 * jb : 8 * jb + 8, :] = v
            return 0

        lax.fori_loop(0, 8 if ib < LB - 1 else 1, gram_row, 0)

    shared(r_x, rx_send, rx_recv, NX, xpos, at_x)
    r_z[zpos] = functools.reduce(jnp.add, [r_x[p] for p in range(NX)])
    share(r_z, rz_send, rz_recv, NZ, zpos, at_z)

    def blk(jb):
        return slice(8 * jb, 8 * jb + 8)

    for kb in range(LB):
        rows_here = 8 if kb < LB - 1 else 1
        for kk in range(rows_here):
            k = kb * 8 + kk
            rinv = 1.0 / a_ref[k, k : k + 1, :]
            dinv[k : k + 1, :] = rinv
            if k == LDEG:
                break
            upper = {jb: a_ref[k, blk(jb), :] for jb in range(kb, LB)}
            lower = {jb: w_ref[k, blk(jb), :] for jb in range(kb + 1)}
            factor = {jb: upper[jb] * rinv for jb in range(kb, LB)}
            for jb in range(kb, LB):
                pf_ref[kk, blk(jb), :] = factor[jb]
            for ii in range(kk + 1, rows_here):
                f = factor[kb][ii : ii + 1]
                for jb in range(kb, LB):
                    a_ref[kb * 8 + ii, blk(jb), :] -= f * upper[jb]
                for jb in range(kb + 1):
                    w_ref[kb * 8 + ii, blk(jb), :] -= f * lower[jb]
        for ib in range(kb + 1, LB):

            def trail(r, _, ib=ib, kb=kb):
                i = ib * 8 + r
                f = [pf_ref[kk, pl.ds(i, 1), :] for kk in range(8)]
                for jb in range(ib, LB):
                    v = a_ref[i, blk(jb), :]
                    for kk in range(8):
                        v = v - f[kk] * a_ref[kb * 8 + kk, blk(jb), :]
                    a_ref[i, blk(jb), :] = v
                for jb in range(kb + 1):
                    v = w_ref[i, blk(jb), :]
                    for kk in range(8):
                        v = v - f[kk] * w_ref[kb * 8 + kk, blk(jb), :]
                    w_ref[i, blk(jb), :] = v
                return 0

            lax.fori_loop(0, 8 if ib < LB - 1 else 1, trail, 0)

    shared(r_z, rz_send, rz_recv, NZ, zpos, at_z)
    r_ag[ycpos] = functools.reduce(jnp.add, [r_z[p] for p in range(NZ)])
    share(r_ag, rag_send, rag_recv, NYC, ycpos, at_yc)
    shared(r_ag, rag_send, rag_recv, NYC, ycpos, at_yc)

    rhs = [r_ag[q // 2, (q % 2) * 8 : (q % 2) * 8 + 8, :] for q in range(2 * LB)]
    xs = (zero,) * (2 * LB)
    for ib in range(LB):

        def back(r, xs, ib=ib):
            i = ib * 8 + r
            xs = list(xs)
            rows = [w_ref[i, blk(jb), :] for jb in range(ib + 1)]
            d = dinv[pl.ds(i, 1), :]
            for part in range(2):
                t = rows[0] * rhs[part * LB]
                for jb in range(1, ib + 1):
                    t = t + rows[jb] * rhs[part * LB + jb]
                s = jnp.sum(t, axis=0, keepdims=True) * d
                for jb in range(ib + 1):
                    xs[part * LB + jb] = xs[part * LB + jb] + rows[jb] * s
            return tuple(xs)

        xs = lax.fori_loop(0, 8 if ib < LB - 1 else 1, back, xs)

    scale = math.sqrt(TEMPLATES)
    for part in range(2):
        full = jnp.concatenate(
            [x * scale for x in xs[part * LB : (part + 1) * LB]]
            + [jnp.zeros((LANES - LPAD, LANES), F32)],
            axis=0,
        ).T
        for s in range(SHELLS):
            out_ref[:, s, part, :] = full[s * ORDERS : (s + 1) * ORDERS, :LROWS]

    sent(st_buf, st_send, st_recv, NY, ypos, at_y)
    sent(m_yc, myc_send, myc_recv, NYC, ycpos, at_yc)
    sent(m_x, mx_send, mx_recv, NX, xpos, at_x)
    sent(m_z, mz_send, mz_recv, NZ, zpos, at_z)
    for d, p in enumerate(peers(NYC, ycpos)):
        remote(
            rhs_ref.at[p], r_yc.at[ycpos], ryc_send.at[d], ryc_recv.at[ycpos], at_yc(p)
        ).wait_send()
    sent(r_x, rx_send, rx_recv, NX, xpos, at_x)
    sent(r_z, rz_send, rz_recv, NZ, zpos, at_z)
    sent(r_ag, rag_send, rag_recv, NYC, ycpos, at_yc)


def body(images, templates, rotation, tilt, inplane, group, precision, radius_bin):
    t_count = templates.shape[0]
    rows = t_count // LANES
    chunks = t_count // CHUNK
    spread, packed, phases = constant_tables()
    vmem = pl.BlockSpec(memory_space=pltpu.VMEM)
    smem = pl.BlockSpec(memory_space=pltpu.SMEM)
    hbm = pl.BlockSpec(memory_space=pl.ANY)
    dma = pltpu.SemaphoreType.DMA
    coeffs, loglik = pl.pallas_call(
        kernel,
        out_shape=(
            jax.ShapeDtypeStruct((ORDERS, SHELLS, 2, LROWS), F32),
            jax.ShapeDtypeStruct((1, LANES), F32),
        ),
        in_specs=[vmem, vmem, vmem, vmem, smem, smem, vmem, vmem, hbm, hbm, hbm],
        out_specs=(vmem, vmem),
        scratch_shapes=[
            pltpu.VMEM((t_count, COEFS), BF16),
            pltpu.VMEM((NTILT, LPAD, LANES), F32),
            pltpu.VMEM((NTILT // 4, LPAD, LANES), F32),
            pltpu.VMEM((NTILT // 4, LPAD, LANES), F32),
            pltpu.VMEM((t_count, LANES), F32),
            pltpu.VMEM((t_count, 2 * LANES), F32),
            pltpu.VMEM((chunks, NTILT, LANES), F32),
            pltpu.VMEM((LANES, LANES), F32),
            pltpu.VMEM((2 * chunks, LANES), F32),
            pltpu.VMEM((LPAD, LPAD, LANES), F32),
            pltpu.VMEM((LPAD, LPAD, LANES), F32),
            pltpu.VMEM((8, LPAD, LANES), F32),
            pltpu.VMEM((LPAD, LANES), F32),
            pltpu.VMEM((2, NTILT, LANES), F32),
            pltpu.VMEM((NYC, 16, LANES), F32),
            pltpu.VMEM((NY, 8, LANES), F32),
            pltpu.VMEM((NYC, 8, LANES), F32),
            pltpu.VMEM((NX, 8, LANES), F32),
            pltpu.VMEM((NZ, 8, LANES), F32),
            pltpu.VMEM((NYC, 16, LANES), F32),
            pltpu.VMEM((NX, 16, LANES), F32),
            pltpu.VMEM((NZ, 16, LANES), F32),
            pltpu.VMEM((NYC, 16, LANES), F32),
            dma((chunks,)),
            dma((2,)),
            dma((NY - 1,)),
            dma((NY,)),
            dma((NYC - 1,)),
            dma((NYC,)),
            dma((NX - 1,)),
            dma((NX,)),
            dma((NZ - 1,)),
            dma((NZ,)),
            dma((NYC - 1,)),
            dma((NYC,)),
            dma((NX - 1,)),
            dma((NX,)),
            dma((NZ - 1,)),
            dma((NZ,)),
            dma((NYC - 1,)),
            dma((NYC,)),
        ],
        compiler_params=pltpu.CompilerParams(collective_id=0, has_side_effects=True),
        name="estep",
    )(
        tilt.reshape(rows, LANES),
        rotation.reshape(rows, LANES),
        inplane.reshape(rows, LANES),
        group.reshape(1, LANES),
        precision,
        radius_bin,
        jnp.asarray(phases),
        images,
        jnp.asarray(spread),
        jnp.asarray(packed),
        templates,
    )
    return coeffs, loglik.reshape(LANES)


def solution(mesh):
    in_specs = (
        P("img", None),
        P(("tpa", "tpb"), None),
        P(("tpa", "tpb")),
        P(("tpa", "tpb")),
        P(("tpa", "tpb")),
        P("img"),
        P(),
        P(),
    )
    out_specs = (P(), P("img"))
    return jax.shard_map(body, mesh=mesh, in_specs=in_specs, out_specs=out_specs, check_vma=False)
```

time: 1050 us -> 55.3 us (0.05)
  other arithmetic: 752 us -> 0 us
  waiting for transfers between devices: 133 us -> 0 us
  blocking collectives: 97.4 us -> 0 us
  Pallas kernels: 0 us -> 51.7 us
  local copies, waits for them, and re-layouts: 27.7 us -> 2.74 us
  matrix products: 23.8 us -> 0 us
  between operations: 15.3 us -> 0.64 us
    another operation x9 -> x0, other arithmetic: 730 us -> none  [the longest x4 580 us: solve_shells(): factor = jnp.linalg.cholesky(gram)]
    reduce_scatter x1 -> x0, waiting for transfers between devices: 133 us -> none  [body(): lax.psum_scatter(lax.dot_general(images, posterior, (((0,), (0,)), ((), (...]
    psum x2 -> x0, blocking collectives: 87.5 us -> none  [the longest x1 80.3 us: body(): lax.psum((right_side, bin_mass), ('img', 'tpa', 'tpb'))]
    pallas_call x0 -> x1, Pallas kernels: none -> 51.7 us  [body(): pl.pallas_call(kernel, out_shape=(jax.ShapeDtypeStruct((ORDERS, SHELLS, 2...]
    another operation x5 -> x0, local copies, waits for them, and re-layouts: 15.6 us -> none  [the longest x1 5.91 us: solve_shells(): jax.scipy.linalg.cho_solve((factor_one, True), right_one)]
    dot_general x10 -> x0, matrix products: 12.2 us -> none  [the longest x1 4.69 us: body(): lax.dot_general(images, posterior, (((0,), (0,)), ((), ())), preferred_el...]
    another operation x2 -> x0, matrix products: 11.6 us -> none  [solve_shells(): jax.scipy.linalg.cho_solve((factor_one, True), right_one)]
  transfers between devices with their start and end apart: 1 -> 0, of which waited for: 1 -> 0; matrix products, arithmetic and copies ran while one was open for 2% -> 0% of each run, Pallas kernels for 0% -> 0%
where the time goes in v1:
time: 55.3 us; the launch traced here: 55.1 us
  Pallas kernels  51.7 us (93%)
  local copies, waits for them, and re-layouts  2.74 us (5%)
  between operations  0.64 us (1%)
    pallas_call x1, Pallas kernels, body(): pl.pallas_call(kernel, out_shape=(jax.ShapeDtypeStruct((ORDERS, SHELLS, 2...  51.7 us
    unnamed x2, local copies, waits for them, and re-layouts  2.74 us

profile of v1, /device:TPU:1, one launch (start us, length us, event | category | flops | bytes accessed | tf_op | source)
XLA Modules:
  0.0 55.1 jit_solution(11624357881596149210)
XLA Ops:
  0.6 51.7 %estep.1 = (f32[32,4,2,49]{3,2,1,0:T(2,128)}, f32[1,128]{1,0:T(1,128)}) custom-call(s32[32,128]{1,0:T(8,128)} %bitcast.5, s32[32,128]{1,0:T(8,128)} %bitcast.6, s32[32,128]{1,0:T(8,128)} %bitcast.7, s32[1,128]{1,0:T(1,128)} %bitcast.8, f32[16]{0:T(128)} %prec_ref.1, s32[8]{0:T(128)} %bin_ref.1, bf16[128,256]{1,0:T(8,128)(2,1)} %constant.6.clone.phase_ref, ...), custom_call_target="tpu_custom_call" | custom-call | tf_op jit(solution)/shard_map/estep/pallas_call | solution.py:545
  52.4 1.6 %copy.15 = f32[32,4,2,49]{3,2,1,0:T(2,128)} copy(f32[32,4,2,49]{3,2,1,0:T(2,128)} %get-tuple-element.8) | data formatting | bytes 100352
  53.9 1.2 %copy.16 = f32[128]{0:T(128)} copy(f32[128]{0:T(128)} %bitcast.9) | data formatting | bytes 1024

commit v2 on v1

--- a/solution.py
+++ b/solution.py
@@ -19,9 +19,11 @@
 NROT = 32
 NGROUP = 16
 RIDGE = 0.05
+LOG2E = math.log2(math.e)
 
 NX, NZ, NCORE, NY = 4, 8, 2, 4
 NYC = NY * NCORE
+HALF = NTILT // 2
 LANES = 128
 LB = 7
 LPAD = 8 * LB
@@ -60,11 +62,10 @@
 
 def constant_tables():
     legendre = legendre_table().transpose(0, 2, 1)
-    padded = np.zeros((NTILT, LPAD, ORDERS))
-    padded[:, :LROWS] = legendre
+    padded = np.zeros((HALF, LPAD, ORDERS))
+    padded[:, :LROWS] = legendre[:HALF]
     spread = np.tile(padded, (1, 1, SHELLS)).astype(np.float32)
-    quarter = NTILT // 4
-    packed = np.concatenate([padded[q * quarter : (q + 1) * quarter] for q in range(4)], axis=2)
+    packed = np.concatenate([padded[q * 8 : q * 8 + 8] for q in range(4)], axis=2)
     packed = packed.astype(np.float32)
     step = np.arange(NROT)[:, None] * np.arange(ORDERS)[None, :] % NROT
     turn = 2.0 * np.pi * step / NROT
@@ -90,6 +91,15 @@
 
 def dot_t(a, b):
     return lax.dot_general(a, b, (((1,), (1,)), ((), ())), preferred_element_type=F32)
+
+
+def by_two(step, count):
+    def pair(i, _):
+        step(2 * i)
+        step(2 * i + 1)
+        return 0
+
+    lax.fori_loop(0, count // 2, pair, 0)
 
 
 def kernel(
@@ -211,10 +221,10 @@
             pl.semaphore_signal(barrier, inc=1, device_id=at(p), device_id_type=MESH)
 
     def tpl_copy(b):
-        rows = pl.ds(pl.multiple_of(b * CHUNK, CHUNK), CHUNK)
+        rows = pl.ds(pl.multiple_of(b * 2 * CHUNK, 2 * CHUNK), 2 * CHUNK)
         return pltpu.make_async_copy(templates_hbm.at[rows], tpl.at[rows], tpl_sem.at[b])
 
-    for b in range(chunks):
+    for b in range(chunks // 2):
         tpl_copy(b).start()
     lt_copy = pltpu.make_async_copy(lt_hbm, lt, tab_sem.at[0])
     lq_copy = pltpu.make_async_copy(lq_hbm, lq, tab_sem.at[1])
@@ -227,7 +237,7 @@
     weight = jnp.zeros((1, LANES), F32)
     for g in range(NGROUP):
         weight = jnp.where(group == g, prec_ref[g], weight)
-    weight = weight * (COEFS ** -0.5)
+    weight = weight * (COEFS ** -0.5 * LOG2E)
 
     c_id = lax.broadcasted_iota(I32, (COEFS, LANES), 0)
     radial = lax.rem(lax.div(c_id, 2), RADII)
@@ -251,10 +261,9 @@
     angle = lax.rem(rot_ref[...] + inp_ref[...], NROT).astype(F32)
     rows_t = angle.shape[0]
     angle = jnp.concatenate([angle, jnp.zeros((LANES - rows_t, LANES), F32)], axis=0)
-    angle_t[...] = angle.T
-
-    def score_chunk(b, _):
-        tpl_copy(b).wait()
+    angle_t[...] = angle.T.astype(BF16)
+
+    def score_chunk(b):
         rows = pl.ds(pl.multiple_of(b * CHUNK, CHUNK), CHUNK)
         block = tpl[rows, :]
         raw = dot_t(block, images)
@@ -262,18 +271,23 @@
         half = 0.5 * jnp.sum(wide * wide, axis=1, keepdims=True)
         score = (raw - half) * weight
         top = jnp.max(score, axis=0, keepdims=True)
-        e = jnp.exp(score - top)
+        e = jnp.exp2(score - top)
         e_ref[rows, :] = e
         cmax[pl.ds(b, 1), :] = top
         cmax[pl.ds(chunks + b, 1), :] = jnp.sum(e, axis=0, keepdims=True)
+
+    def score_pair(i, _):
+        tpl_copy(i).wait()
+        score_chunk(2 * i)
+        score_chunk(2 * i + 1)
         return 0
 
-    lax.fori_loop(0, chunks, score_chunk, 0)
+    lax.fori_loop(0, chunks // 2, score_pair, 0)
 
     tops = cmax[pl.ds(0, chunks), :]
     sums = cmax[pl.ds(chunks, chunks), :]
     top = jnp.max(tops, axis=0, keepdims=True)
-    total = jnp.sum(sums * jnp.exp(tops - top), axis=0, keepdims=True)
+    total = jnp.sum(sums * jnp.exp2(tops - top), axis=0, keepdims=True)
     row8 = lax.broadcasted_iota(I32, (8, LANES), 0)
     st_buf[ypos] = jnp.where(row8 == 0, top, total)
 
@@ -284,38 +298,38 @@
         tilt = jnp.concatenate(
             [tilt_ref[pl.ds(2 * b, 1), :], tilt_ref[pl.ds(2 * b + 1, 1), :]], axis=1
         )
-        k_id = lax.broadcasted_iota(I32, (NTILT, CHUNK), 0)
+        row = lax.broadcasted_iota(I32, (NTILT, CHUNK), 0)
+        k_id = jnp.where(row < HALF, row, NTILT + HALF - 1 - row)
         return jnp.where(k_id == tilt, 1.0, 0.0).astype(BF16)
 
-    lane_sq = lax.broadcasted_iota(I32, (LANES, LANES), 1)
-
-    def prepare_chunk(b, _):
+    row_pick = lax.broadcasted_iota(I32, (LANES, 2 * LANES), 0)
+    lane_half = lax.div(lax.broadcasted_iota(I32, (LANES, 2 * LANES), 1), LANES)
+    lane_turn = lax.rem(lax.broadcasted_iota(I32, (LANES, LANES), 1), NROT).astype(F32)
+
+    def prepare_chunk(b):
         rows = pl.ds(pl.multiple_of(b * CHUNK, CHUNK), CHUNK)
-        hots = []
-        for h in range(2):
-            picked = jnp.sum(
-                jnp.where(lane_sq == 2 * b + h, angle_t[...], 0.0), axis=1, keepdims=True
-            )
-            hots.append(
-                jnp.where(lax.rem(lane_sq, NROT) == picked.astype(I32), 1.0, 0.0).astype(BF16)
-            )
+        pick = jnp.where(row_pick == lane_half + 2 * b, 1.0, 0.0).astype(BF16)
+        spread = dot(angle_t[...], pick)
+        hots = [
+            jnp.where(spread[:, h * LANES : (h + 1) * LANES] == lane_turn, 1.0, 0.0).astype(BF16)
+            for h in range(2)
+        ]
         ph_ref[rows, :] = dot(jnp.concatenate(hots, axis=0), phase_ref[...])
         e_high, e_low = split2(e_ref[rows, :])
         both = dot(tilt_hot(b), jnp.concatenate([e_high, e_low], axis=1))
         emass[b] = both[:, :LANES] + both[:, LANES:]
-        return 0
-
-    lax.fori_loop(0, chunks, prepare_chunk, 0)
+
+    by_two(prepare_chunk, chunks)
 
     shared(st_buf, st_send, st_recv, NY, ypos, at_y)
     stats = [st_buf[p] for p in range(NY)]
     all_top = functools.reduce(jnp.maximum, [s[0:1] for s in stats])
     all_sum = functools.reduce(
-        jnp.add, [s[1:2] * jnp.exp(s[0:1] - all_top) for s in stats]
+        jnp.add, [s[1:2] * jnp.exp2(s[0:1] - all_top) for s in stats]
     )
-    loglik = all_top + jnp.log(all_sum)
-    loglik_ref[...] = loglik
-    scales = jnp.exp(tops - loglik)
+    log_sum = jnp.log(all_sum)
+    loglik_ref[...] = all_top * math.log(2.0) + log_sum
+    scales = jnp.exp2((tops - all_top) - log_sum * LOG2E)
     cmax[pl.ds(0, chunks), :] = scales
 
     mass = jnp.zeros((NTILT, LANES), F32)
@@ -323,43 +337,44 @@
         mass = mass + emass[b] * scales[b : b + 1]
     mass = jnp.broadcast_to(jnp.sum(mass, axis=1, keepdims=True), (NTILT, LANES))
     packed = jnp.zeros((8, LANES), F32)
-    for a in range(8):
-        packed = jnp.where(lax.div(lane, 16) == a, mass[8 * a : 8 * a + 8], packed)
+    for q in range(4):
+        for h in range(2):
+            start = h * HALF + 8 * q
+            packed = jnp.where(lax.div(lane, 16) == 2 * q + h, mass[start : start + 8], packed)
     m_yc[ycpos] = packed
     share(m_yc, myc_send, myc_recv, NYC, ycpos, at_yc)
 
     bins_ref[...] = jnp.zeros_like(bins_ref)
 
-    def post_chunk(b, _):
-        rows = pl.ds(pl.multiple_of(b * CHUNK, CHUNK), CHUNK)
-        posterior = (e_ref[rows, :] * cmax[pl.ds(b, 1), :]).astype(BF16)
-        weighted = dot(jnp.concatenate([posterior, posterior], axis=1), shelled)
-        real, imag = weighted[:, :LANES], weighted[:, LANES:]
-        cosine, sine = ph_ref[rows, :LANES], ph_ref[rows, LANES:]
-        rotated = jnp.concatenate(
-            [real * cosine + imag * sine, imag * cosine - real * sine], axis=1
-        )
-        high, low = split2(rotated)
-        hot = tilt_hot(b)
-        both = dot(hot, high) + dot(hot, low)
+    def post_chunk(i, _):
+        highs, lows, hots = [], [], []
+        for h in range(2):
+            b = 2 * i + h
+            rows = pl.ds(pl.multiple_of(b * CHUNK, CHUNK), CHUNK)
+            posterior = (e_ref[rows, :] * cmax[pl.ds(b, 1), :]).astype(BF16)
+            weighted = dot(jnp.concatenate([posterior, posterior], axis=1), shelled)
+            real, imag = weighted[:, :LANES], weighted[:, LANES:]
+            cosine, sine = ph_ref[rows, :LANES], ph_ref[rows, LANES:]
+            rotated = jnp.concatenate(
+                [real * cosine + imag * sine, imag * cosine - real * sine], axis=1
+            )
+            high, low = split2(rotated)
+            highs.append(high)
+            lows.append(low)
+            hots.append(tilt_hot(b))
+        hot = jnp.concatenate(hots, axis=1)
+        both = dot(hot, jnp.concatenate(highs, axis=0)) + dot(hot, jnp.concatenate(lows, axis=0))
         bins_ref[0] += both[:, :LANES]
         bins_ref[1] += both[:, LANES:]
         return 0
 
-    half_way = chunks // 2
-    lax.fori_loop(0, half_way, post_chunk, 0)
-
-    shared(m_yc, myc_send, myc_recv, NYC, ycpos, at_yc)
-    m_x[xpos] = functools.reduce(jnp.add, [m_yc[p] for p in range(NYC)])
-    share(m_x, mx_send, mx_recv, NX, xpos, at_x)
-
-    lax.fori_loop(half_way, chunks, post_chunk, 0)
-
-    shared(m_x, mx_send, mx_recv, NX, xpos, at_x)
-    m_z[zpos] = functools.reduce(jnp.add, [m_x[p] for p in range(NX)])
-    share(m_z, mz_send, mz_recv, NZ, zpos, at_z)
+    lax.fori_loop(0, chunks // 2, post_chunk, 0)
 
     lt_copy.wait()
+
+    sub8 = lax.broadcasted_iota(I32, (8, LANES), 0)
+    lane8 = lax.broadcasted_iota(I32, (8, LANES), 1)
+    even = lax.rem(sub8 + lane8, 2) == 0
 
     def project(k8, accs):
         accs = list(accs)
@@ -367,14 +382,16 @@
             k = k8 * 8 + dk
             for part in range(2):
                 row = bins_ref[part, pl.ds(k, 1), :]
+                mirror = bins_ref[part, pl.ds(HALF + k, 1), :]
+                folded = jnp.where(even, row + mirror, row - mirror)
                 for jb in range(LB):
                     accs[part * LB + jb] = (
-                        accs[part * LB + jb] + lt[k, 8 * jb : 8 * jb + 8, :] * row
+                        accs[part * LB + jb] + lt[k, 8 * jb : 8 * jb + 8, :] * folded
                     )
         return tuple(accs)
 
     zero = jnp.zeros((8, LANES), F32)
-    accs = lax.fori_loop(0, NTILT // 8, project, (zero,) * (2 * LB))
+    accs = lax.fori_loop(0, HALF // 8, project, (zero,) * (2 * LB))
     for q in range(2 * NYC):
         rhs_ref[q // 2, (q % 2) * 8 : (q % 2) * 8 + 8, :] = accs[q] if q < 2 * LB else zero
 
@@ -384,8 +401,11 @@
             rhs_ref.at[p], r_yc.at[ycpos], ryc_send.at[d], ryc_recv.at[ycpos], at_yc(p)
         ).start()
 
+    shared(m_yc, myc_send, myc_recv, NYC, ycpos, at_yc)
+    m_x[xpos] = functools.reduce(jnp.add, [m_yc[p] for p in range(NYC)])
+    share(m_x, mx_send, mx_recv, NX, xpos, at_x)
+
     lq_copy.wait()
-    sub8 = lax.broadcasted_iota(I32, (8, LANES), 0)
     for jb in range(LB):
         for ib in range(LB):
             if jb <= ib:
@@ -398,51 +418,62 @@
     r_x[xpos] = functools.reduce(jnp.add, [r_yc[p] for p in range(NYC)])
     share(r_x, rx_send, rx_recv, NX, xpos, at_x)
 
+    shared(m_x, mx_send, mx_recv, NX, xpos, at_x)
+    m_z[zpos] = functools.reduce(jnp.add, [m_x[p] for p in range(NX)])
+    share(m_z, mz_send, mz_recv, NZ, zpos, at_z)
+
+    shared(r_x, rx_send, rx_recv, NX, xpos, at_x)
+    r_z[zpos] = functools.reduce(jnp.add, [r_x[p] for p in range(NX)])
+    share(r_z, rz_send, rz_recv, NZ, zpos, at_z)
+
     shared(m_z, mz_send, mz_recv, NZ, zpos, at_z)
     pm = functools.reduce(jnp.add, [m_z[p] for p in range(NZ)])
     mean_mass = jnp.sum(jnp.sum(pm, axis=0, keepdims=True), axis=1, keepdims=True) / (
         16.0 * NTILT
     )
     first_half = lax.rem(lane, 32) < 16
-    mass_h = (
-        jnp.where(first_half, pm, pltpu.roll(pm, 16, 1)),
-        jnp.where(first_half, pltpu.roll(pm, LANES - 16, 1), pm),
-    )
+    near = jnp.where(first_half, pm, pltpu.roll(pm, 16, 1))
+    far = jnp.where(first_half, pltpu.roll(pm, LANES - 16, 1), pm)
+    both_mass, diff_mass = near + far, near - far
     shell_lane = lax.div(lane, ORDERS)
     count = jnp.zeros((1, LANES), F32)
     for p in range(RADII):
         count = count + jnp.where(shell_lane == bin_ref[p], 1.0, 0.0)
     ridge = (RIDGE * mean_mass) * (count + 1.0)
-    quarter = NTILT // 4
-    for k in range(quarter):
-        for jb in range(LB):
-            mlq[k, 8 * jb : 8 * jb + 8, :] = (
-                lq[k, 8 * jb : 8 * jb + 8, :] * mass_h[k // 8][k % 8 : k % 8 + 1]
-            )
+    sub_even = lax.rem(sub8, 2) == 0
+    for k in range(8):
+        plus, minus = both_mass[k : k + 1], diff_mass[k : k + 1]
+        for parity in range(2):
+            signed = jnp.where(sub_even, minus, plus) if parity else jnp.where(sub_even, plus, minus)
+            for jb in range(LB):
+                mlq[parity * 8 + k, 8 * jb : 8 * jb + 8, :] = (
+                    lq[k, 8 * jb : 8 * jb + 8, :] * signed
+                )
     for ib in range(LB):
 
-        def gram_row(r, _, ib=ib):
-            i = ib * 8 + r
-            acc = [zero] * LB
-            for k in range(quarter):
-                row = mlq[k, pl.ds(i, 1), :]
+        def gram_rows(h, _, ib=ib):
+            group = 4 if ib < LB - 1 else 1
+            first = ib * 8 + h * 4
+            acc = [[zero] * LB for _ in range(group)]
+            for k in range(8):
+                rows = [lq[k, pl.ds(first + r, 1), :] for r in range(group)]
                 for jb in range(ib, LB):
-                    acc[jb] = acc[jb] + lq[k, 8 * jb : 8 * jb + 8, :] * row
+                    for parity in range(min(group, 2)):
+                        term = mlq[parity * 8 + k, 8 * jb : 8 * jb + 8, :]
+                        for r in range(parity, group, 2):
+                            acc[r][jb] = acc[r][jb] + term * rows[r]
             for jb in range(ib, LB):
-                v = acc[jb]
-                v = v + pltpu.roll(v, 32, 1)
-                v = v + pltpu.roll(v, 64, 1)
-                v = v * count
-                if jb == ib:
-                    v = v + jnp.where(sub8 == r, ridge, 0.0)
-                a_ref[i, 8 * jb : 8 * jb + 8, :] = v
+                for r in range(group):
+                    v = acc[r][jb]
+                    v = v + pltpu.roll(v, 32, 1)
+                    v = v + pltpu.roll(v, 64, 1)
+                    v = v * count
+                    if jb == ib:
+                        v = v + jnp.where(sub8 == h * 4 + r, ridge, 0.0)
+                    a_ref[first + r, 8 * jb : 8 * jb + 8, :] = v
             return 0
 
-        lax.fori_loop(0, 8 if ib < LB - 1 else 1, gram_row, 0)
-
-    shared(r_x, rx_send, rx_recv, NX, xpos, at_x)
-    r_z[zpos] = functools.reduce(jnp.add, [r_x[p] for p in range(NX)])
-    share(r_z, rz_send, rz_recv, NZ, zpos, at_z)
+        lax.fori_loop(0, 2 if ib < LB - 1 else 1, gram_rows, 0)
 
     def blk(jb):
         return slice(8 * jb, 8 * jb + 8)
@@ -468,26 +499,38 @@
                     w_ref[kb * 8 + ii, blk(jb), :] -= f * lower[jb]
         for ib in range(kb + 1, LB):
 
-            def trail(r, _, ib=ib, kb=kb):
-                i = ib * 8 + r
-                f = [pf_ref[kk, pl.ds(i, 1), :] for kk in range(8)]
-                for jb in range(ib, LB):
-                    v = a_ref[i, blk(jb), :]
-                    for kk in range(8):
-                        v = v - f[kk] * a_ref[kb * 8 + kk, blk(jb), :]
-                    a_ref[i, blk(jb), :] = v
-                for jb in range(kb + 1):
-                    v = w_ref[i, blk(jb), :]
-                    for kk in range(8):
-                        v = v - f[kk] * w_ref[kb * 8 + kk, blk(jb), :]
-                    w_ref[i, blk(jb), :] = v
+            def trail(h, _, ib=ib, kb=kb):
+                group = 4 if ib < LB - 1 else 1
+                first = ib * 8 + h * 4
+                f = [
+                    [pf_ref[kk, pl.ds(first + r, 1), :] for r in range(group)] for kk in range(8)
+                ]
+                for ref, blocks in ((a_ref, range(ib, LB)), (w_ref, range(kb + 1))):
+                    for jb in blocks:
+                        v = [ref[first + r, blk(jb), :] for r in range(group)]
+                        for kk in range(8):
+                            u = ref[kb * 8 + kk, blk(jb), :]
+                            v = [v[r] - f[kk][r] * u for r in range(group)]
+                        for r in range(group):
+                            ref[first + r, blk(jb), :] = v[r]
                 return 0
 
-            lax.fori_loop(0, 8 if ib < LB - 1 else 1, trail, 0)
-
-    shared(r_z, rz_send, rz_recv, NZ, zpos, at_z)
-    r_ag[ycpos] = functools.reduce(jnp.add, [r_z[p] for p in range(NZ)])
-    share(r_ag, rag_send, rag_recv, NYC, ycpos, at_yc)
+            lax.fori_loop(0, 2 if ib < LB - 1 else 1, trail, 0)
+        if kb == 1:
+            shared(r_z, rz_send, rz_recv, NZ, zpos, at_z)
+            r_ag[ycpos] = functools.reduce(jnp.add, [r_z[p] for p in range(NZ)])
+            share(r_ag, rag_send, rag_recv, NYC, ycpos, at_yc)
+
+    sent(st_buf, st_send, st_recv, NY, ypos, at_y)
+    sent(m_yc, myc_send, myc_recv, NYC, ycpos, at_yc)
+    sent(m_x, mx_send, mx_recv, NX, xpos, at_x)
+    sent(m_z, mz_send, mz_recv, NZ, zpos, at_z)
+    for d, p in enumerate(peers(NYC, ycpos)):
+        remote(
+            rhs_ref.at[p], r_yc.at[ycpos], ryc_send.at[d], ryc_recv.at[ycpos], at_yc(p)
+        ).wait_send()
+    sent(r_x, rx_send, rx_recv, NX, xpos, at_x)
+    sent(r_z, rz_send, rz_recv, NZ, zpos, at_z)
     shared(r_ag, rag_send, rag_recv, NYC, ycpos, at_yc)
 
     rhs = [r_ag[q // 2, (q % 2) * 8 : (q % 2) * 8 + 8, :] for q in range(2 * LB)]
@@ -511,26 +554,19 @@
         xs = lax.fori_loop(0, 8 if ib < LB - 1 else 1, back, xs)
 
     scale = math.sqrt(TEMPLATES)
+    for q in range(2 * LB):
+        out_ref[q // LB, blk(q % LB), :] = xs[q] * scale
+
+    sent(r_ag, rag_send, rag_recv, NYC, ycpos, at_yc)
+
+
+def arrange(x_ref, row_ref, out_ref, loglik_ref):
+    loglik_ref[...] = row_ref[...]
+    pad = jnp.zeros((LANES - LPAD, LANES), F32)
     for part in range(2):
-        full = jnp.concatenate(
-            [x * scale for x in xs[part * LB : (part + 1) * LB]]
-            + [jnp.zeros((LANES - LPAD, LANES), F32)],
-            axis=0,
-        ).T
+        full = jnp.concatenate([x_ref[part], pad], axis=0).T
         for s in range(SHELLS):
             out_ref[:, s, part, :] = full[s * ORDERS : (s + 1) * ORDERS, :LROWS]
-
-    sent(st_buf, st_send, st_recv, NY, ypos, at_y)
-    sent(m_yc, myc_send, myc_recv, NYC, ycpos, at_yc)
-    sent(m_x, mx_send, mx_recv, NX, xpos, at_x)
-    sent(m_z, mz_send, mz_recv, NZ, zpos, at_z)
-    for d, p in enumerate(peers(NYC, ycpos)):
-        remote(
-            rhs_ref.at[p], r_yc.at[ycpos], ryc_send.at[d], ryc_recv.at[ycpos], at_yc(p)
-        ).wait_send()
-    sent(r_x, rx_send, rx_recv, NX, xpos, at_x)
-    sent(r_z, rz_send, rz_recv, NZ, zpos, at_z)
-    sent(r_ag, rag_send, rag_recv, NYC, ycpos, at_yc)
 
 
 def body(images, templates, rotation, tilt, inplane, group, precision, radius_bin):
@@ -542,23 +578,23 @@
     smem = pl.BlockSpec(memory_space=pltpu.SMEM)
     hbm = pl.BlockSpec(memory_space=pl.ANY)
     dma = pltpu.SemaphoreType.DMA
-    coeffs, loglik = pl.pallas_call(
+    solved, row = pl.pallas_call(
         kernel,
         out_shape=(
-            jax.ShapeDtypeStruct((ORDERS, SHELLS, 2, LROWS), F32),
+            jax.ShapeDtypeStruct((2, LPAD, LANES), F32),
             jax.ShapeDtypeStruct((1, LANES), F32),
         ),
         in_specs=[vmem, vmem, vmem, vmem, smem, smem, vmem, vmem, hbm, hbm, hbm],
         out_specs=(vmem, vmem),
         scratch_shapes=[
             pltpu.VMEM((t_count, COEFS), BF16),
-            pltpu.VMEM((NTILT, LPAD, LANES), F32),
-            pltpu.VMEM((NTILT // 4, LPAD, LANES), F32),
-            pltpu.VMEM((NTILT // 4, LPAD, LANES), F32),
+            pltpu.VMEM((HALF, LPAD, LANES), F32),
+            pltpu.VMEM((8, LPAD, LANES), F32),
+            pltpu.VMEM((16, LPAD, LANES), F32),
             pltpu.VMEM((t_count, LANES), F32),
             pltpu.VMEM((t_count, 2 * LANES), F32),
             pltpu.VMEM((chunks, NTILT, LANES), F32),
-            pltpu.VMEM((LANES, LANES), F32),
+            pltpu.VMEM((LANES, LANES), BF16),
             pltpu.VMEM((2 * chunks, LANES), F32),
             pltpu.VMEM((LPAD, LPAD, LANES), F32),
             pltpu.VMEM((LPAD, LPAD, LANES), F32),
@@ -574,7 +610,7 @@
             pltpu.VMEM((NX, 16, LANES), F32),
             pltpu.VMEM((NZ, 16, LANES), F32),
             pltpu.VMEM((NYC, 16, LANES), F32),
-            dma((chunks,)),
+            dma((chunks // 2,)),
             dma((2,)),
             dma((NY - 1,)),
             dma((NY,)),
@@ -608,6 +644,16 @@
         jnp.asarray(packed),
         templates,
     )
+    coeffs, loglik = pl.pallas_call(
+        arrange,
+        out_shape=(
+            jax.ShapeDtypeStruct((ORDERS, SHELLS, 2, LROWS), F32),
+            jax.ShapeDtypeStruct((1, LANES), F32),
+        ),
+        in_specs=[vmem, vmem],
+        out_specs=(vmem, vmem),
+        name="arrange",
+    )(solved, row)
     return coeffs, loglik.reshape(LANES)
 
 

time: 55.3 us -> 41.9 us (0.76)
  Pallas kernels: 51.7 us -> 41.1 us
  local copies, waits for them, and re-layouts: 2.74 us -> 0 us
    pallas_call x1 -> x2, Pallas kernels: 51.7 us -> 41.1 us  [the longest x1 39.5 us: body(): pl.pallas_call(kernel, out_shape=(jax.ShapeDtypeStruct((2, LPAD, LANES),...]
    unnamed x2 -> x0, local copies, waits for them, and re-layouts: 2.74 us -> none
where the time goes in v2:
time: 41.9 us; the launch traced here: 41.8 us
  Pallas kernels  41.1 us (98%)
  between operations  0.64 us (2%)
    pallas_call x1, Pallas kernels, body(): pl.pallas_call(kernel, out_shape=(jax.ShapeDtypeStruct((2, LPAD, LANES),...  39.5 us
    pallas_call x1, Pallas kernels, body(): pl.pallas_call(arrange, out_shape=(jax.ShapeDtypeStruct((ORDERS, SHELLS,...  1.62 us

profile of v2, /device:TPU:1, one launch (start us, length us, event | category | flops | bytes accessed | tf_op | source)
XLA Modules:
  0.0 41.8 jit_solution(8728083258778327916)
XLA Ops:
  0.6 39.5 %estep.1 = (f32[2,56,128]{2,1,0:T(8,128)}, f32[1,128]{1,0:T(1,128)}) custom-call(s32[32,128]{1,0:T(8,128)} %bitcast.5, s32[32,128]{1,0:T(8,128)} %bitcast.6, s32[32,128]{1,0:T(8,128)} %bitcast.7, s32[1,128]{1,0:T(1,128)} %bitcast.8, f32[16]{0:T(128)} %prec_ref.1, s32[8]{0:T(128)} %bin_ref.1, bf16[128,256]{1,0:T(8,128)(2,1)} %constant.6.clone.phase_ref, ...), custom_call_target="tpu_custom_call" | custom-call | tf_op jit(solution)/shard_map/estep/pallas_call | solution.py:581
  40.2 1.6 %arrange.1 = (f32[32,4,2,49]{3,2,1,0:T(2,128)}, f32[1,128]{1,0:T(1,128)}) custom-call(f32[2,56,128]{2,1,0:T(8,128)} %get-tuple-element.6.x_ref, f32[1,128]{1,0:T(1,128)} %get-tuple-element.7.row_ref), custom_call_target="tpu_custom_call" | custom-call | tf_op jit(solution)/shard_map/arrange/pallas_call | solution.py:647

commit v3 on v2

--- a/solution.py
+++ b/solution.py
@@ -23,12 +23,15 @@
 
 NX, NZ, NCORE, NY = 4, 8, 2, 4
 NYC = NY * NCORE
+NZC = NZ * NCORE
+NXY = NX * NY
 HALF = NTILT // 2
 LANES = 128
 LB = 7
 LPAD = 8 * LB
 LROWS = LDEG + 1
-CHUNK = 256
+CHUNK = 512
+CUTS = CHUNK // LANES
 F32, BF16, I32 = jnp.float32, jnp.bfloat16, jnp.int32
 MESH = pl.DeviceIdType.MESH
 
@@ -93,29 +96,29 @@
     return lax.dot_general(a, b, (((1,), (1,)), ((), ())), preferred_element_type=F32)
 
 
-def by_two(step, count):
-    def pair(i, _):
-        step(2 * i)
-        step(2 * i + 1)
-        return 0
-
-    lax.fori_loop(0, count // 2, pair, 0)
-
-
 def kernel(
-    tilt_ref,
-    rot_ref,
-    inp_ref,
+    tilt_hbm,
+    rot_hbm,
+    inp_hbm,
     group_ref,
     prec_ref,
     bin_ref,
-    phase_ref,
-    images_ref,
+    phase_hbm,
+    images_hbm,
     lt_hbm,
     lq_hbm,
     templates_hbm,
     out_ref,
     loglik_ref,
+    tilt_ref,
+    rot_ref,
+    inp_ref,
+    phase_ref,
+    images_ref,
+    raw_buf,
+    score_buf,
+    high_buf,
+    low_buf,
     tpl,
     lt,
     lq,
@@ -132,9 +135,8 @@
     bins_ref,
     rhs_ref,
     st_buf,
-    m_yc,
-    m_x,
-    m_z,
+    m_zc,
+    m_xy,
     r_yc,
     r_x,
     r_z,
@@ -143,12 +145,10 @@
     tab_sem,
     st_send,
     st_recv,
-    myc_send,
-    myc_recv,
-    mx_send,
-    mx_recv,
-    mz_send,
-    mz_recv,
+    mzc_send,
+    mzc_recv,
+    mxy_send,
+    mxy_recv,
     ryc_send,
     ryc_recv,
     rx_send,
@@ -167,28 +167,33 @@
     zpos = lax.rem(lax.div(img, NCORE), NZ)
     xpos = lax.div(img, NCORE * NZ)
     ypos = tpa * 2 + tpb
-    ycpos = ypos * NCORE + core
+    ycpos = core * NY + ypos
+
+    zcpos = zpos * NCORE + core
+    xypos = xpos * NY + ypos
+    chip = img - core
+    column = img - zcpos
+
+    def device(at_img, y):
+        return {"img": at_img, "tpa": lax.div(y, 2), "tpb": lax.rem(y, 2)}
 
     def at_y(p):
-        return {"img": img, "tpa": lax.div(p, 2), "tpb": lax.rem(p, 2)}
+        return device(img, p)
 
     def at_yc(p):
-        y = lax.div(p, NCORE)
-        return {
-            "img": lax.div(img, NCORE) * NCORE + lax.rem(p, NCORE),
-            "tpa": lax.div(y, 2),
-            "tpb": lax.rem(y, 2),
-        }
+        return device(chip + lax.div(p, NY), lax.rem(p, NY))
 
     def at_x(p):
-        return {"img": p * (NZ * NCORE) + lax.rem(img, NZ * NCORE), "tpa": tpa, "tpb": tpb}
+        return {"img": p * NZC + zcpos, "tpa": tpa, "tpb": tpb}
 
     def at_z(p):
-        return {
-            "img": lax.div(img, NZ * NCORE) * (NZ * NCORE) + p * NCORE + core,
-            "tpa": tpa,
-            "tpb": tpb,
-        }
+        return {"img": column + p * NCORE + core, "tpa": tpa, "tpb": tpb}
+
+    def at_zc(p):
+        return {"img": column + p, "tpa": tpa, "tpb": tpb}
+
+    def at_xy(p):
+        return device(lax.div(p, NY) * NZC + zcpos, lax.rem(p, NY))
 
     def peers(n, me):
         return [lax.rem(me + d, n) for d in range(1, n)]
@@ -215,74 +220,88 @@
         for d, p in enumerate(peers(n, me)):
             remote(buf.at[me], buf.at[me], send.at[d], recv.at[me], at(p)).wait_send()
 
+    def tpl_copy(b):
+        rows = pl.ds(b * CHUNK, CHUNK)
+        return pltpu.make_async_copy(templates_hbm.at[rows], tpl.at[rows], tpl_sem.at[b])
+
+    operands = (
+        (images_hbm, images_ref),
+        (tilt_hbm, tilt_ref),
+        (rot_hbm, rot_ref),
+        (inp_hbm, inp_ref),
+        (phase_hbm, phase_ref),
+        (lt_hbm, lt),
+        (lq_hbm, lq),
+    )
+    copies = [
+        pltpu.make_async_copy(src, dst, tab_sem.at[i]) for i, (src, dst) in enumerate(operands)
+    ]
+    copies[0].start()
+    for b in range(chunks):
+        tpl_copy(b).start()
+    for copy in copies[1:]:
+        copy.start()
+
     barrier = pltpu.get_barrier_semaphore()
-    for n, me, at in ((NYC, ycpos, at_yc), (NX, xpos, at_x), (NZ, zpos, at_z)):
-        for p in peers(n, me):
-            pl.semaphore_signal(barrier, inc=1, device_id=at(p), device_id_type=MESH)
-
-    def tpl_copy(b):
-        rows = pl.ds(pl.multiple_of(b * 2 * CHUNK, 2 * CHUNK), 2 * CHUNK)
-        return pltpu.make_async_copy(templates_hbm.at[rows], tpl.at[rows], tpl_sem.at[b])
-
-    for b in range(chunks // 2):
-        tpl_copy(b).start()
-    lt_copy = pltpu.make_async_copy(lt_hbm, lt, tab_sem.at[0])
-    lq_copy = pltpu.make_async_copy(lq_hbm, lq, tab_sem.at[1])
-    lt_copy.start()
-    lq_copy.start()
+    greeted = [at_zc(p) for p in peers(NZC, zcpos)] + [at_xy(p) for p in peers(NXY, xypos)]
+    greeted += [device(chip + 1 - core, p) for p in peers(NY, ypos)]
+    for target in greeted:
+        pl.semaphore_signal(barrier, inc=1, device_id=target, device_id_type=MESH)
 
     lane = lax.broadcasted_iota(I32, (1, LANES), 1)
 
+    copies[0].wait()
     group = group_ref[...]
     weight = jnp.zeros((1, LANES), F32)
     for g in range(NGROUP):
         weight = jnp.where(group == g, prec_ref[g], weight)
     weight = weight * (COEFS ** -0.5 * LOG2E)
 
-    c_id = lax.broadcasted_iota(I32, (COEFS, LANES), 0)
-    radial = lax.rem(lax.div(c_id, 2), RADII)
-    shell_of = jnp.zeros((COEFS, LANES), I32)
+    r_id = lax.broadcasted_iota(I32, (16, LANES), 0)
+    l_id = lax.broadcasted_iota(I32, (16, LANES), 1)
+    order_at = l_id
     for p in range(RADII):
-        shell_of = jnp.where(radial == p, bin_ref[p], shell_of)
-    column = shell_of * ORDERS + lax.div(c_id, 2 * RADII)
-    hit = column == lax.broadcasted_iota(I32, (COEFS, LANES), 1)
-    part_of = lax.rem(c_id, 2)
+        order_at = jnp.where(lax.div(r_id, 2) == p, l_id - ORDERS * bin_ref[p], order_at)
+    order_of = [jnp.where(lax.rem(r_id, 2) == part, order_at, -1) for part in range(2)]
     select = jnp.concatenate(
         [
-            jnp.where(jnp.logical_and(hit, part_of == 0), 1.0, 0.0),
-            jnp.where(jnp.logical_and(hit, part_of == 1), 1.0, 0.0),
+            jnp.concatenate([jnp.where(o == m, 1.0, 0.0).astype(BF16) for o in order_of], axis=1)
+            for m in range(ORDERS)
         ],
-        axis=1,
-    ).astype(BF16)
+        axis=0,
+    )
     images = images_ref[...]
     img_high, img_low = split2(dot(images, select))
     shelled = jnp.concatenate([img_high, img_low], axis=0)
 
-    angle = lax.rem(rot_ref[...] + inp_ref[...], NROT).astype(F32)
-    rows_t = angle.shape[0]
-    angle = jnp.concatenate([angle, jnp.zeros((LANES - rows_t, LANES), F32)], axis=0)
-    angle_t[...] = angle.T.astype(BF16)
-
-    def score_chunk(b):
-        rows = pl.ds(pl.multiple_of(b * CHUNK, CHUNK), CHUNK)
-        block = tpl[rows, :]
-        raw = dot_t(block, images)
-        wide = block.astype(F32)
+    def chunk_rows(b):
+        return pl.ds(b * CHUNK if isinstance(b, int) else pl.multiple_of(b * CHUNK, CHUNK), CHUNK)
+
+    def raw_stage(b):
+        raw_buf[:, :LANES] = dot_t(tpl[chunk_rows(b), :], images)
+
+    def score_stage(b):
+        wide = tpl[chunk_rows(b), :].astype(F32)
         half = 0.5 * jnp.sum(wide * wide, axis=1, keepdims=True)
-        score = (raw - half) * weight
-        top = jnp.max(score, axis=0, keepdims=True)
-        e = jnp.exp2(score - top)
-        e_ref[rows, :] = e
-        cmax[pl.ds(b, 1), :] = top
+        score = (raw_buf[:, :LANES] - half) * weight
+        score_buf[...] = score
+        cmax[pl.ds(b, 1), :] = jnp.max(score, axis=0, keepdims=True)
+
+    def exp_stage(b):
+        e = jnp.exp2(score_buf[...] - cmax[pl.ds(b, 1), :])
+        e_ref[chunk_rows(b), :] = e
         cmax[pl.ds(chunks + b, 1), :] = jnp.sum(e, axis=0, keepdims=True)
 
-    def score_pair(i, _):
-        tpl_copy(i).wait()
-        score_chunk(2 * i)
-        score_chunk(2 * i + 1)
-        return 0
-
-    lax.fori_loop(0, chunks // 2, score_pair, 0)
+    waits = {0: (0,), 1: (1,), 2: (2, 3), 4: tuple(range(4, chunks))}
+    for step in range(chunks + 2):
+        for b in waits.get(step, ()):
+            tpl_copy(b).wait()
+        if step >= 2:
+            exp_stage(step - 2)
+        if 1 <= step <= chunks:
+            score_stage(step - 1)
+        if step < chunks:
+            raw_stage(step)
 
     tops = cmax[pl.ds(0, chunks), :]
     sums = cmax[pl.ds(chunks, chunks), :]
@@ -291,35 +310,44 @@
     row8 = lax.broadcasted_iota(I32, (8, LANES), 0)
     st_buf[ypos] = jnp.where(row8 == 0, top, total)
 
-    pl.semaphore_wait(barrier, (NYC - 1) + (NX - 1) + (NZ - 1))
+    pl.semaphore_wait(barrier, (NZC - 1) + (NXY - 1) + (NY - 1))
     share(st_buf, st_send, st_recv, NY, ypos, at_y)
+
+    for copy in copies[1:5]:
+        copy.wait()
+
+    angle = lax.rem(rot_ref[...] + inp_ref[...], NROT).astype(F32)
+    rows_t = angle.shape[0]
+    angle = jnp.concatenate([angle, jnp.zeros((LANES - rows_t, LANES), F32)], axis=0)
+    angle_t[...] = angle.T.astype(BF16)
 
     def tilt_hot(b):
         tilt = jnp.concatenate(
-            [tilt_ref[pl.ds(2 * b, 1), :], tilt_ref[pl.ds(2 * b + 1, 1), :]], axis=1
+            [tilt_ref[pl.ds(CUTS * b + h, 1), :] for h in range(CUTS)], axis=1
         )
         row = lax.broadcasted_iota(I32, (NTILT, CHUNK), 0)
         k_id = jnp.where(row < HALF, row, NTILT + HALF - 1 - row)
         return jnp.where(k_id == tilt, 1.0, 0.0).astype(BF16)
 
-    row_pick = lax.broadcasted_iota(I32, (LANES, 2 * LANES), 0)
-    lane_half = lax.div(lax.broadcasted_iota(I32, (LANES, 2 * LANES), 1), LANES)
+    row_pick = lax.broadcasted_iota(I32, (LANES, CHUNK), 0)
+    lane_half = lax.div(lax.broadcasted_iota(I32, (LANES, CHUNK), 1), LANES)
     lane_turn = lax.rem(lax.broadcasted_iota(I32, (LANES, LANES), 1), NROT).astype(F32)
 
-    def prepare_chunk(b):
-        rows = pl.ds(pl.multiple_of(b * CHUNK, CHUNK), CHUNK)
-        pick = jnp.where(row_pick == lane_half + 2 * b, 1.0, 0.0).astype(BF16)
+    def prepare_chunk(b, _):
+        rows = chunk_rows(b)
+        pick = jnp.where(row_pick == lane_half + CUTS * b, 1.0, 0.0).astype(BF16)
         spread = dot(angle_t[...], pick)
         hots = [
             jnp.where(spread[:, h * LANES : (h + 1) * LANES] == lane_turn, 1.0, 0.0).astype(BF16)
-            for h in range(2)
+            for h in range(CUTS)
         ]
         ph_ref[rows, :] = dot(jnp.concatenate(hots, axis=0), phase_ref[...])
         e_high, e_low = split2(e_ref[rows, :])
         both = dot(tilt_hot(b), jnp.concatenate([e_high, e_low], axis=1))
         emass[b] = both[:, :LANES] + both[:, LANES:]
-
-    by_two(prepare_chunk, chunks)
+        return 0
+
+    lax.fori_loop(0, chunks, prepare_chunk, 0)
 
     shared(st_buf, st_send, st_recv, NY, ypos, at_y)
     stats = [st_buf[p] for p in range(NY)]
@@ -341,36 +369,39 @@
         for h in range(2):
             start = h * HALF + 8 * q
             packed = jnp.where(lax.div(lane, 16) == 2 * q + h, mass[start : start + 8], packed)
-    m_yc[ycpos] = packed
-    share(m_yc, myc_send, myc_recv, NYC, ycpos, at_yc)
-
-    bins_ref[...] = jnp.zeros_like(bins_ref)
-
-    def post_chunk(i, _):
-        highs, lows, hots = [], [], []
-        for h in range(2):
-            b = 2 * i + h
-            rows = pl.ds(pl.multiple_of(b * CHUNK, CHUNK), CHUNK)
-            posterior = (e_ref[rows, :] * cmax[pl.ds(b, 1), :]).astype(BF16)
-            weighted = dot(jnp.concatenate([posterior, posterior], axis=1), shelled)
-            real, imag = weighted[:, :LANES], weighted[:, LANES:]
-            cosine, sine = ph_ref[rows, :LANES], ph_ref[rows, LANES:]
-            rotated = jnp.concatenate(
-                [real * cosine + imag * sine, imag * cosine - real * sine], axis=1
-            )
-            high, low = split2(rotated)
-            highs.append(high)
-            lows.append(low)
-            hots.append(tilt_hot(b))
-        hot = jnp.concatenate(hots, axis=1)
-        both = dot(hot, jnp.concatenate(highs, axis=0)) + dot(hot, jnp.concatenate(lows, axis=0))
-        bins_ref[0] += both[:, :LANES]
-        bins_ref[1] += both[:, LANES:]
-        return 0
-
-    lax.fori_loop(0, chunks // 2, post_chunk, 0)
-
-    lt_copy.wait()
+    m_zc[zcpos] = packed
+    share(m_zc, mzc_send, mzc_recv, NZC, zcpos, at_zc)
+
+
+    def weighted_stage(b):
+        posterior = (e_ref[chunk_rows(b), :] * cmax[pl.ds(b, 1), :]).astype(BF16)
+        raw_buf[...] = dot(jnp.concatenate([posterior, posterior], axis=1), shelled)
+
+    def rotate_stage(b):
+        rows = chunk_rows(b)
+        real, imag = raw_buf[:, :LANES], raw_buf[:, LANES:]
+        cosine, sine = ph_ref[rows, :LANES], ph_ref[rows, LANES:]
+        for part, turned in enumerate((real * cosine + imag * sine, imag * cosine - real * sine)):
+            high, low = split2(turned)
+            high_buf[:, part * LANES : (part + 1) * LANES] = high
+            low_buf[:, part * LANES : (part + 1) * LANES] = low
+
+    def tilt_stage(b):
+        hot = tilt_hot(b)
+        return dot(hot, high_buf[...]) + dot(hot, low_buf[...])
+
+    binned = jnp.zeros((NTILT, 2 * LANES), F32)
+    for step in range(chunks + 2):
+        if step >= 2:
+            binned = binned + tilt_stage(step - 2)
+        if 1 <= step <= chunks:
+            rotate_stage(step - 1)
+        if step < chunks:
+            weighted_stage(step)
+    bins_ref[0] = binned[:, :LANES]
+    bins_ref[1] = binned[:, LANES:]
+
+    copies[5].wait()
 
     sub8 = lax.broadcasted_iota(I32, (8, LANES), 0)
     lane8 = lax.broadcasted_iota(I32, (8, LANES), 1)
@@ -401,11 +432,11 @@
             rhs_ref.at[p], r_yc.at[ycpos], ryc_send.at[d], ryc_recv.at[ycpos], at_yc(p)
         ).start()
 
-    shared(m_yc, myc_send, myc_recv, NYC, ycpos, at_yc)
-    m_x[xpos] = functools.reduce(jnp.add, [m_yc[p] for p in range(NYC)])
-    share(m_x, mx_send, mx_recv, NX, xpos, at_x)
-
-    lq_copy.wait()
+    shared(m_zc, mzc_send, mzc_recv, NZC, zcpos, at_zc)
+    m_xy[xypos] = functools.reduce(jnp.add, [m_zc[p] for p in range(NZC)])
+    share(m_xy, mxy_send, mxy_recv, NXY, xypos, at_xy)
+
+    copies[6].wait()
     for jb in range(LB):
         for ib in range(LB):
             if jb <= ib:
@@ -418,16 +449,12 @@
     r_x[xpos] = functools.reduce(jnp.add, [r_yc[p] for p in range(NYC)])
     share(r_x, rx_send, rx_recv, NX, xpos, at_x)
 
-    shared(m_x, mx_send, mx_recv, NX, xpos, at_x)
-    m_z[zpos] = functools.reduce(jnp.add, [m_x[p] for p in range(NX)])
-    share(m_z, mz_send, mz_recv, NZ, zpos, at_z)
-
     shared(r_x, rx_send, rx_recv, NX, xpos, at_x)
     r_z[zpos] = functools.reduce(jnp.add, [r_x[p] for p in range(NX)])
     share(r_z, rz_send, rz_recv, NZ, zpos, at_z)
 
-    shared(m_z, mz_send, mz_recv, NZ, zpos, at_z)
-    pm = functools.reduce(jnp.add, [m_z[p] for p in range(NZ)])
+    shared(m_xy, mxy_send, mxy_recv, NXY, xypos, at_xy)
+    pm = functools.reduce(jnp.add, [m_xy[p] for p in range(NXY)])
     mean_mass = jnp.sum(jnp.sum(pm, axis=0, keepdims=True), axis=1, keepdims=True) / (
         16.0 * NTILT
     )
@@ -516,15 +543,14 @@
                 return 0
 
             lax.fori_loop(0, 2 if ib < LB - 1 else 1, trail, 0)
-        if kb == 1:
+        if kb == 0:
             shared(r_z, rz_send, rz_recv, NZ, zpos, at_z)
             r_ag[ycpos] = functools.reduce(jnp.add, [r_z[p] for p in range(NZ)])
             share(r_ag, rag_send, rag_recv, NYC, ycpos, at_yc)
 
     sent(st_buf, st_send, st_recv, NY, ypos, at_y)
-    sent(m_yc, myc_send, myc_recv, NYC, ycpos, at_yc)
-    sent(m_x, mx_send, mx_recv, NX, xpos, at_x)
-    sent(m_z, mz_send, mz_recv, NZ, zpos, at_z)
+    sent(m_zc, mzc_send, mzc_recv, NZC, zcpos, at_zc)
+    sent(m_xy, mxy_send, mxy_recv, NXY, xypos, at_xy)
     for d, p in enumerate(peers(NYC, ycpos)):
         remote(
             rhs_ref.at[p], r_yc.at[ycpos], ryc_send.at[d], ryc_recv.at[ycpos], at_yc(p)
@@ -581,12 +607,21 @@
     solved, row = pl.pallas_call(
         kernel,
         out_shape=(
-            jax.ShapeDtypeStruct((2, LPAD, LANES), F32),
-            jax.ShapeDtypeStruct((1, LANES), F32),
+            pltpu.VMEM((2, LPAD, LANES), F32),
+            pltpu.VMEM((1, LANES), F32),
         ),
-        in_specs=[vmem, vmem, vmem, vmem, smem, smem, vmem, vmem, hbm, hbm, hbm],
+        in_specs=[hbm, hbm, hbm, vmem, smem, smem, hbm, hbm, hbm, hbm, hbm],
         out_specs=(vmem, vmem),
         scratch_shapes=[
+            pltpu.VMEM((rows, LANES), I32),
+            pltpu.VMEM((rows, LANES), I32),
+            pltpu.VMEM((rows, LANES), I32),
+            pltpu.VMEM(phases.shape, BF16),
+            pltpu.VMEM(images.shape, BF16),
+            pltpu.VMEM((CHUNK, 2 * LANES), F32),
+            pltpu.VMEM((CHUNK, LANES), F32),
+            pltpu.VMEM((CHUNK, 2 * LANES), BF16),
+            pltpu.VMEM((CHUNK, 2 * LANES), BF16),
             pltpu.VMEM((t_count, COEFS), BF16),
             pltpu.VMEM((HALF, LPAD, LANES), F32),
             pltpu.VMEM((8, LPAD, LANES), F32),
@@ -603,23 +638,20 @@
             pltpu.VMEM((2, NTILT, LANES), F32),
             pltpu.VMEM((NYC, 16, LANES), F32),
             pltpu.VMEM((NY, 8, LANES), F32),
-            pltpu.VMEM((NYC, 8, LANES), F32),
-            pltpu.VMEM((NX, 8, LANES), F32),
-            pltpu.VMEM((NZ, 8, LANES), F32),
+            pltpu.VMEM((NZC, 8, LANES), F32),
+            pltpu.VMEM((NXY, 8, LANES), F32),
             pltpu.VMEM((NYC, 16, LANES), F32),
             pltpu.VMEM((NX, 16, LANES), F32),
             pltpu.VMEM((NZ, 16, LANES), F32),
             pltpu.VMEM((NYC, 16, LANES), F32),
-            dma((chunks // 2,)),
-            dma((2,)),
+            dma((chunks,)),
+            dma((7,)),
             dma((NY - 1,)),
             dma((NY,)),
-            dma((NYC - 1,)),
-            dma((NYC,)),
-            dma((NX - 1,)),
-            dma((NX,)),
-            dma((NZ - 1,)),
-            dma((NZ,)),
+            dma((NZC - 1,)),
+            dma((NZC,)),
+            dma((NXY - 1,)),
+            dma((NXY,)),
             dma((NYC - 1,)),
             dma((NYC,)),
             dma((NX - 1,)),
@@ -653,7 +685,10 @@
         in_specs=[vmem, vmem],
         out_specs=(vmem, vmem),
         name="arrange",
-    )(solved, row)
+    )(
+        pltpu.with_memory_space_constraint(solved, pltpu.VMEM),
+        pltpu.with_memory_space_constraint(row, pltpu.VMEM),
+    )
     return coeffs, loglik.reshape(LANES)
 
 

time: 41.9 us -> 37.1 us (0.89)
  Pallas kernels: 41.1 us -> 36.4 us
    pallas_call x1, Pallas kernels: 39.5 us -> 35.6 us  [body(): pl.pallas_call(kernel, out_shape=(pltpu.VMEM((2, LPAD, LANES), F32), pltp...]
    pallas_call x1, Pallas kernels: 1.62 us -> 0.8 us  [body(): pl.pallas_call(arrange, out_shape=(jax.ShapeDtypeStruct((ORDERS, SHELLS,...]
where the time goes in v3:
time: 37.1 us; the launch traced here: 37 us
  Pallas kernels  36.4 us (98%)
  between operations  0.64 us (2%)
    pallas_call x1, Pallas kernels, body(): pl.pallas_call(kernel, out_shape=(pltpu.VMEM((2, LPAD, LANES), F32), pltp...  35.6 us
    pallas_call x1, Pallas kernels, body(): pl.pallas_call(arrange, out_shape=(jax.ShapeDtypeStruct((ORDERS, SHELLS,...  0.8 us

profile of v3, /device:TPU:1, one launch (start us, length us, event | category | flops | bytes accessed | tf_op | source)
XLA Modules:
  0.0 37.0 jit_solution(11727086956312788679)
XLA Ops:
  0.6 35.6 %estep.1 = (f32[2,56,128]{2,1,0:T(8,128)S(1)}, f32[1,128]{1,0:T(1,128)S(1)}) custom-call(s32[32,128]{1,0:T(8,128)} %bitcast.5, s32[32,128]{1,0:T(8,128)} %bitcast.6, s32[32,128]{1,0:T(8,128)} %bitcast.7, s32[1,128]{1,0:T(1,128)} %bitcast.8, f32[16]{0:T(128)} %prec_ref.1, s32[8]{0:T(128)} %bin_ref.1, bf16[128,256]{1,0:T(8,128)(2,1)} %constant.6.clone.phase_hbm, ...), custom_call_target="tpu_custom_call" | custom-call | tf_op jit(solution)/shard_map/estep/pallas_call | solution.py:607
  36.2 0.8 %arrange.1 = (f32[32,4,2,49]{3,2,1,0:T(2,128)}, f32[1,128]{1,0:T(1,128)}) custom-call(f32[2,56,128]{2,1,0:T(8,128)S(1)} %get-tuple-element.6.x_ref, f32[1,128]{1,0:T(1,128)S(1)} %get-tuple-element.7.row_ref), custom_call_target="tpu_custom_call" | custom-call | tf_op jit(solution)/shard_map/arrange/pallas_call | solution.py:679

commit v4 on v3

--- a/solution.py
+++ b/solution.py
@@ -360,18 +360,6 @@
     scales = jnp.exp2((tops - all_top) - log_sum * LOG2E)
     cmax[pl.ds(0, chunks), :] = scales
 
-    mass = jnp.zeros((NTILT, LANES), F32)
-    for b in range(chunks):
-        mass = mass + emass[b] * scales[b : b + 1]
-    mass = jnp.broadcast_to(jnp.sum(mass, axis=1, keepdims=True), (NTILT, LANES))
-    packed = jnp.zeros((8, LANES), F32)
-    for q in range(4):
-        for h in range(2):
-            start = h * HALF + 8 * q
-            packed = jnp.where(lax.div(lane, 16) == 2 * q + h, mass[start : start + 8], packed)
-    m_zc[zcpos] = packed
-    share(m_zc, mzc_send, mzc_recv, NZC, zcpos, at_zc)
-
 
     def weighted_stage(b):
         posterior = (e_ref[chunk_rows(b), :] * cmax[pl.ds(b, 1), :]).astype(BF16)
@@ -432,9 +420,17 @@
             rhs_ref.at[p], r_yc.at[ycpos], ryc_send.at[d], ryc_recv.at[ycpos], at_yc(p)
         ).start()
 
-    shared(m_zc, mzc_send, mzc_recv, NZC, zcpos, at_zc)
-    m_xy[xypos] = functools.reduce(jnp.add, [m_zc[p] for p in range(NZC)])
-    share(m_xy, mxy_send, mxy_recv, NXY, xypos, at_xy)
+    mass = jnp.zeros((NTILT, LANES), F32)
+    for b in range(chunks):
+        mass = mass + emass[b] * scales[b : b + 1]
+    mass = jnp.broadcast_to(jnp.sum(mass, axis=1, keepdims=True), (NTILT, LANES))
+    packed = jnp.zeros((8, LANES), F32)
+    for q in range(4):
+        for h in range(2):
+            start = h * HALF + 8 * q
+            packed = jnp.where(lax.div(lane, 16) == 2 * q + h, mass[start : start + 8], packed)
+    m_zc[zcpos] = packed
+    share(m_zc, mzc_send, mzc_recv, NZC, zcpos, at_zc)
 
     copies[6].wait()
     for jb in range(LB):
@@ -448,6 +444,10 @@
     shared(r_yc, ryc_send, ryc_recv, NYC, ycpos, at_yc)
     r_x[xpos] = functools.reduce(jnp.add, [r_yc[p] for p in range(NYC)])
     share(r_x, rx_send, rx_recv, NX, xpos, at_x)
+
+    shared(m_zc, mzc_send, mzc_recv, NZC, zcpos, at_zc)
+    m_xy[xypos] = functools.reduce(jnp.add, [m_zc[p] for p in range(NZC)])
+    share(m_xy, mxy_send, mxy_recv, NXY, xypos, at_xy)
 
     shared(r_x, rx_send, rx_recv, NX, xpos, at_x)
     r_z[zpos] = functools.reduce(jnp.add, [r_x[p] for p in range(NX)])
@@ -502,6 +502,10 @@
 
         lax.fori_loop(0, 2 if ib < LB - 1 else 1, gram_rows, 0)
 
+    shared(r_z, rz_send, rz_recv, NZ, zpos, at_z)
+    r_ag[ycpos] = functools.reduce(jnp.add, [r_z[p] for p in range(NZ)])
+    share(r_ag, rag_send, rag_recv, NYC, ycpos, at_yc)
+
     def blk(jb):
         return slice(8 * jb, 8 * jb + 8)
 
@@ -543,10 +547,6 @@
                 return 0
 
             lax.fori_loop(0, 2 if ib < LB - 1 else 1, trail, 0)
-        if kb == 0:
-            shared(r_z, rz_send, rz_recv, NZ, zpos, at_z)
-            r_ag[ycpos] = functools.reduce(jnp.add, [r_z[p] for p in range(NZ)])
-            share(r_ag, rag_send, rag_recv, NYC, ycpos, at_yc)
 
     sent(st_buf, st_send, st_recv, NY, ypos, at_y)
     sent(m_zc, mzc_send, mzc_recv, NZC, zcpos, at_zc)
@@ -560,24 +560,17 @@
     shared(r_ag, rag_send, rag_recv, NYC, ycpos, at_yc)
 
     rhs = [r_ag[q // 2, (q % 2) * 8 : (q % 2) * 8 + 8, :] for q in range(2 * LB)]
-    xs = (zero,) * (2 * LB)
-    for ib in range(LB):
-
-        def back(r, xs, ib=ib):
-            i = ib * 8 + r
-            xs = list(xs)
-            rows = [w_ref[i, blk(jb), :] for jb in range(ib + 1)]
-            d = dinv[pl.ds(i, 1), :]
-            for part in range(2):
-                t = rows[0] * rhs[part * LB]
-                for jb in range(1, ib + 1):
-                    t = t + rows[jb] * rhs[part * LB + jb]
-                s = jnp.sum(t, axis=0, keepdims=True) * d
-                for jb in range(ib + 1):
-                    xs[part * LB + jb] = xs[part * LB + jb] + rows[jb] * s
-            return tuple(xs)
-
-        xs = lax.fori_loop(0, 8 if ib < LB - 1 else 1, back, xs)
+    xs = [zero] * (2 * LB)
+    for i in range(LROWS):
+        ib = i // 8
+        rows = [w_ref[i, blk(jb), :] for jb in range(ib + 1)]
+        for part in range(2):
+            t = rows[0] * rhs[part * LB]
+            for jb in range(1, ib + 1):
+                t = t + rows[jb] * rhs[part * LB + jb]
+            s = jnp.sum(t, axis=0, keepdims=True) * dinv[i : i + 1, :]
+            for jb in range(ib + 1):
+                xs[part * LB + jb] = xs[part * LB + jb] + rows[jb] * s
 
     scale = math.sqrt(TEMPLATES)
     for q in range(2 * LB):

time: 37.1 us -> 36.8 us (level)
  no operation moved by 1% of the time
where the time goes in v4:
time: 36.8 us; the launch traced here: 36.7 us
  Pallas kernels  36.1 us (98%)
  between operations  0.64 us (2%)
    pallas_call x1, Pallas kernels, body(): pl.pallas_call(kernel, out_shape=(pltpu.VMEM((2, LPAD, LANES), F32), pltp...  35.3 us
    pallas_call x1, Pallas kernels, body(): pl.pallas_call(arrange, out_shape=(jax.ShapeDtypeStruct((ORDERS, SHELLS,...  0.8 us

profile of v4, /device:TPU:1, one launch (start us, length us, event | category | flops | bytes accessed | tf_op | source)
XLA Modules:
  0.0 36.7 jit_solution(15300050646689035148)
XLA Ops:
  0.6 35.3 %estep.1 = (f32[2,56,128]{2,1,0:T(8,128)S(1)}, f32[1,128]{1,0:T(1,128)S(1)}) custom-call(s32[32,128]{1,0:T(8,128)} %bitcast.5, s32[32,128]{1,0:T(8,128)} %bitcast.6, s32[32,128]{1,0:T(8,128)} %bitcast.7, s32[1,128]{1,0:T(1,128)} %bitcast.8, f32[16]{0:T(128)} %prec_ref.1, s32[8]{0:T(128)} %bin_ref.1, bf16[128,256]{1,0:T(8,128)(2,1)} %constant.6.clone.phase_hbm, ...), custom_call_target="tpu_custom_call" | custom-call | tf_op jit(solution)/shard_map/estep/pallas_call | solution.py:600
  35.9 0.8 %arrange.1 = (f32[32,4,2,49]{3,2,1,0:T(2,128)}, f32[1,128]{1,0:T(1,128)}) custom-call(f32[2,56,128]{2,1,0:T(8,128)S(1)} %get-tuple-element.6.x_ref, f32[1,128]{1,0:T(1,128)S(1)} %get-tuple-element.7.row_ref), custom_call_target="tpu_custom_call" | custom-call | tf_op jit(solution)/shard_map/arrange/pallas_call | solution.py:672

commit v5 on v4

--- a/solution.py
+++ b/solution.py
@@ -100,9 +100,9 @@
     tilt_hbm,
     rot_hbm,
     inp_hbm,
-    group_ref,
-    prec_ref,
-    bin_ref,
+    group_hbm,
+    prec_hbm,
+    radius_hbm,
     phase_hbm,
     images_hbm,
     lt_hbm,
@@ -113,6 +113,9 @@
     tilt_ref,
     rot_ref,
     inp_ref,
+    group_ref,
+    prec_ref,
+    radius_ref,
     phase_ref,
     images_ref,
     raw_buf,
@@ -166,7 +169,7 @@
     core = lax.rem(img, NCORE)
     zpos = lax.rem(lax.div(img, NCORE), NZ)
     xpos = lax.div(img, NCORE * NZ)
-    ypos = tpa * 2 + tpb
+    ypos = tpb * 2 + tpa
     ycpos = core * NY + ypos
 
     zcpos = zpos * NCORE + core
@@ -175,7 +178,7 @@
     column = img - zcpos
 
     def device(at_img, y):
-        return {"img": at_img, "tpa": lax.div(y, 2), "tpb": lax.rem(y, 2)}
+        return {"img": at_img, "tpa": lax.rem(y, 2), "tpb": lax.div(y, 2)}
 
     def at_y(p):
         return device(img, p)
@@ -196,7 +199,11 @@
         return device(lax.div(p, NY) * NZC + zcpos, lax.rem(p, NY))
 
     def peers(n, me):
-        return [lax.rem(me + d, n) for d in range(1, n)]
+        if n == NYC and me is ycpos:
+            steps = (2, 6, 1, 3, 5, 7, 4)
+        else:
+            steps = sorted(range(1, n), key=lambda d: -min(d, n - d))
+        return [lax.rem(me + d, n) for d in steps]
 
     def remote(src, dst, send, recv, device):
         return pltpu.make_async_remote_copy(
@@ -232,14 +239,18 @@
         (phase_hbm, phase_ref),
         (lt_hbm, lt),
         (lq_hbm, lq),
+        (group_hbm, group_ref),
+        (prec_hbm, prec_ref),
+        (radius_hbm, radius_ref),
     )
     copies = [
         pltpu.make_async_copy(src, dst, tab_sem.at[i]) for i, (src, dst) in enumerate(operands)
     ]
-    copies[0].start()
+    for i in (7, 8, 9, 0):
+        copies[i].start()
     for b in range(chunks):
         tpl_copy(b).start()
-    for copy in copies[1:]:
+    for copy in copies[1:7]:
         copy.start()
 
     barrier = pltpu.get_barrier_semaphore()
@@ -250,18 +261,19 @@
 
     lane = lax.broadcasted_iota(I32, (1, LANES), 1)
 
-    copies[0].wait()
+    for i in (7, 8, 9, 0):
+        copies[i].wait()
     group = group_ref[...]
     weight = jnp.zeros((1, LANES), F32)
     for g in range(NGROUP):
-        weight = jnp.where(group == g, prec_ref[g], weight)
+        weight = jnp.where(group == g, prec_ref[:, g : g + 1], weight)
     weight = weight * (COEFS ** -0.5 * LOG2E)
 
     r_id = lax.broadcasted_iota(I32, (16, LANES), 0)
     l_id = lax.broadcasted_iota(I32, (16, LANES), 1)
     order_at = l_id
     for p in range(RADII):
-        order_at = jnp.where(lax.div(r_id, 2) == p, l_id - ORDERS * bin_ref[p], order_at)
+        order_at = jnp.where(lax.div(r_id, 2) == p, l_id - ORDERS * radius_ref[:, p : p + 1], order_at)
     order_of = [jnp.where(lax.rem(r_id, 2) == part, order_at, -1) for part in range(2)]
     select = jnp.concatenate(
         [
@@ -465,7 +477,7 @@
     shell_lane = lax.div(lane, ORDERS)
     count = jnp.zeros((1, LANES), F32)
     for p in range(RADII):
-        count = count + jnp.where(shell_lane == bin_ref[p], 1.0, 0.0)
+        count = count + jnp.where(shell_lane == radius_ref[:, p : p + 1], 1.0, 0.0)
     ridge = (RIDGE * mean_mass) * (count + 1.0)
     sub_even = lax.rem(sub8, 2) == 0
     for k in range(8):
@@ -594,7 +606,6 @@
     chunks = t_count // CHUNK
     spread, packed, phases = constant_tables()
     vmem = pl.BlockSpec(memory_space=pltpu.VMEM)
-    smem = pl.BlockSpec(memory_space=pltpu.SMEM)
     hbm = pl.BlockSpec(memory_space=pl.ANY)
     dma = pltpu.SemaphoreType.DMA
     solved, row = pl.pallas_call(
@@ -603,12 +614,15 @@
             pltpu.VMEM((2, LPAD, LANES), F32),
             pltpu.VMEM((1, LANES), F32),
         ),
-        in_specs=[hbm, hbm, hbm, vmem, smem, smem, hbm, hbm, hbm, hbm, hbm],
+        in_specs=[hbm, hbm, hbm, hbm, hbm, hbm, hbm, hbm, hbm, hbm, hbm],
         out_specs=(vmem, vmem),
         scratch_shapes=[
             pltpu.VMEM((rows, LANES), I32),
             pltpu.VMEM((rows, LANES), I32),
             pltpu.VMEM((rows, LANES), I32),
+            pltpu.VMEM((1, LANES), I32),
+            pltpu.VMEM((1, NGROUP), F32),
+            pltpu.VMEM((1, RADII), I32),
             pltpu.VMEM(phases.shape, BF16),
             pltpu.VMEM(images.shape, BF16),
             pltpu.VMEM((CHUNK, 2 * LANES), F32),
@@ -638,7 +652,7 @@
             pltpu.VMEM((NZ, 16, LANES), F32),
             pltpu.VMEM((NYC, 16, LANES), F32),
             dma((chunks,)),
-            dma((7,)),
+            dma((10,)),
             dma((NY - 1,)),
             dma((NY,)),
             dma((NZC - 1,)),
@@ -661,8 +675,8 @@
         rotation.reshape(rows, LANES),
         inplane.reshape(rows, LANES),
         group.reshape(1, LANES),
-        precision,
-        radius_bin,
+        precision.reshape(1, NGROUP),
+        radius_bin.reshape(1, RADII),
         jnp.asarray(phases),
         images,
         jnp.asarray(spread),

time: 36.8 us -> 35.6 us (0.967)
  Pallas kernels: 36.1 us -> 34.9 us
    pallas_call x1, Pallas kernels: 35.3 us -> 34.1 us  [body(): pl.pallas_call(kernel, out_shape=(pltpu.VMEM((2, LPAD, LANES), F32), pltp...]
where the time goes in v5:
time: 35.6 us
  Pallas kernels  34.9 us (98%)
  between operations  0.64 us (2%)
    pallas_call x1, Pallas kernels, body(): pl.pallas_call(kernel, out_shape=(pltpu.VMEM((2, LPAD, LANES), F32), pltp...  34.1 us
    pallas_call x1, Pallas kernels, body(): pl.pallas_call(arrange, out_shape=(jax.ShapeDtypeStruct((ORDERS, SHELLS,...  0.8 us

profile of v5, /device:TPU:1, one launch (start us, length us, event | category | flops | bytes accessed | tf_op | source)
XLA Modules:
  0.0 35.6 jit_solution(935825462573624524)
XLA Ops:
  0.6 34.1 %estep.1 = (f32[2,56,128]{2,1,0:T(8,128)S(1)}, f32[1,128]{1,0:T(1,128)S(1)}) custom-call(s32[32,128]{1,0:T(8,128)} %bitcast.7, s32[32,128]{1,0:T(8,128)} %bitcast.8, s32[32,128]{1,0:T(8,128)} %bitcast.9, s32[1,128]{1,0:T(1,128)} %bitcast.10, f32[1,16]{1,0:T(1,128)} %bitcast.11, s32[1,8]{1,0:T(1,128)} %bitcast.12, bf16[128,256]{1,0:T(8,128)(2,1)} %constant.6.clone.phase_hbm, ...), custom_call_target="tpu_custom_call" | custom-call | tf_op jit(solution)/shard_map/estep/pallas_call | solution.py:611
  34.8 0.8 %arrange.1 = (f32[32,4,2,49]{3,2,1,0:T(2,128)}, f32[1,128]{1,0:T(1,128)}) custom-call(f32[2,56,128]{2,1,0:T(8,128)S(1)} %get-tuple-element.6.x_ref, f32[1,128]{1,0:T(1,128)S(1)} %get-tuple-element.7.row_ref), custom_call_target="tpu_custom_call" | custom-call | tf_op jit(solution)/shard_map/arrange/pallas_call | solution.py:686

commit v6 on v5

--- a/solution.py
+++ b/solution.py
@@ -513,10 +513,10 @@
             return 0
 
         lax.fori_loop(0, 2 if ib < LB - 1 else 1, gram_rows, 0)
-
-    shared(r_z, rz_send, rz_recv, NZ, zpos, at_z)
-    r_ag[ycpos] = functools.reduce(jnp.add, [r_z[p] for p in range(NZ)])
-    share(r_ag, rag_send, rag_recv, NYC, ycpos, at_yc)
+        if ib == 2:
+            shared(r_z, rz_send, rz_recv, NZ, zpos, at_z)
+            r_ag[ycpos] = functools.reduce(jnp.add, [r_z[p] for p in range(NZ)])
+            share(r_ag, rag_send, rag_recv, NYC, ycpos, at_yc)
 
     def blk(jb):
         return slice(8 * jb, 8 * jb + 8)

time: 35.6 us -> 35.2 us (0.989)
  Pallas kernels: 34.9 us -> 34.5 us
    pallas_call x1, Pallas kernels: 34.1 us -> 33.7 us  [body(): pl.pallas_call(kernel, out_shape=(pltpu.VMEM((2, LPAD, LANES), F32), pltp...]
where the time goes in v6:
time: 35.2 us; the launch traced here: 35.1 us
  Pallas kernels  34.5 us (98%)
  between operations  0.64 us (2%)
    pallas_call x1, Pallas kernels, body(): pl.pallas_call(kernel, out_shape=(pltpu.VMEM((2, LPAD, LANES), F32), pltp...  33.7 us
    pallas_call x1, Pallas kernels, body(): pl.pallas_call(arrange, out_shape=(jax.ShapeDtypeStruct((ORDERS, SHELLS,...  0.8 us

profile of v6, /device:TPU:1, one launch (start us, length us, event | category | flops | bytes accessed | tf_op | source)
XLA Modules:
  0.0 35.1 jit_solution(6578883295592749266)
XLA Ops:
  0.6 33.7 %estep.1 = (f32[2,56,128]{2,1,0:T(8,128)S(1)}, f32[1,128]{1,0:T(1,128)S(1)}) custom-call(s32[32,128]{1,0:T(8,128)} %bitcast.7, s32[32,128]{1,0:T(8,128)} %bitcast.8, s32[32,128]{1,0:T(8,128)} %bitcast.9, s32[1,128]{1,0:T(1,128)} %bitcast.10, f32[1,16]{1,0:T(1,128)} %bitcast.11, s32[1,8]{1,0:T(1,128)} %bitcast.12, bf16[128,256]{1,0:T(8,128)(2,1)} %constant.6.clone.phase_hbm, ...), custom_call_target="tpu_custom_call" | custom-call | tf_op jit(solution)/shard_map/estep/pallas_call | solution.py:611
  34.3 0.8 %arrange.1 = (f32[32,4,2,49]{3,2,1,0:T(2,128)}, f32[1,128]{1,0:T(1,128)}) custom-call(f32[2,56,128]{2,1,0:T(8,128)S(1)} %get-tuple-element.6.x_ref, f32[1,128]{1,0:T(1,128)S(1)} %get-tuple-element.7.row_ref), custom_call_target="tpu_custom_call" | custom-call | tf_op jit(solution)/shard_map/arrange/pallas_call | solution.py:686
